TPU v7x, 128 devices: a whole 4x4x4 slice. The times are simulated.
128 devices in a mesh: tm: 8 (over y, core), height: 16 (over x, z).
Axes of the slice: x: 4, y: 4, z: 4, core: 2. Of those that a mesh axis runs over, the one named last changes fastest.
Arguments:
- stream: bfloat16 [8, 64, 160, 2240], P('tm', 'height'), may hold values from -6 to 6
- query_tokens: bfloat16 [8, 64, 160, 1120], P('tm', 'height'), may hold values from -6 to 6
- key_tokens: bfloat16 [8, 64, 160, 1120], P('tm', 'height'), may hold values from -6 to 6
- value_tokens: bfloat16 [8, 64, 160, 1120], P('tm', 'height'), may hold values from -12 to 12
- out_weight: bfloat16 [1120, 2240], replicated, may hold values from -0.1875 to 0.1875
- in_weight: bfloat16 [2240, 2, 2800], P(None, None, 'height'), may hold values from -0.125 to 0.125
- conv_weight: float32 [3, 3, 2, 2800], replicated, may hold values from -1.2 to 1.2
Outputs:
- attended: bfloat16 [8, 64, 160, 1120], P('tm', 'height')
- gated: bfloat16 [8, 64, 160, 2800], P('tm', 'height')
All inputs are finite; a program needn't handle non-finite values.
Results may differ from a plain program's by a relative error of at most 0.0074.
Values may be sent and summed in bfloat16 or wider, within the bound.
A program may use at most 128 MiB of HBM per device.

v0:
```python
import jax
import jax.numpy as jnp
from jax import lax
from jax.sharding import PartitionSpec as P

HD = 112


def cut_along(x, dim, devices):
    lengths = x.shape
    parts = x.reshape(*lengths[:dim], devices, lengths[dim] // devices, *lengths[dim + 1 :])
    return jnp.moveaxis(parts, dim, 0)


def sent_and_summed(x, axis, dim):
    parts = cut_along(x, dim, lax.axis_size(axis))
    arrived = lax.all_to_all(parts, axis, split_axis=0, concat_axis=0, tiled=True)
    return arrived.sum(axis=0)


def sent_together(arrays, axis, dim, along):
    widths = [a.shape[along] for a in arrays]
    both = jnp.concatenate(arrays, axis=along)
    out = sent_and_summed(both, axis, dim)
    return tuple(jnp.split(out, [sum(widths[:k]) for k in range(1, len(widths))], axis=along))


def collected_together(x, axis):
    leaves = jax.tree.leaves(x)
    turns = sorted(range(len(leaves)), key=lambda k: -leaves[k].size)
    width = (1, *leaves[turns[0]].shape)[-1]
    lines = [
        jnp.pad(leaves[k].reshape(-1), (0, -leaves[k].size % width)).reshape(-1, width)
        for k in turns
    ]
    both, at, found = (lax.all_gather(jnp.concatenate(lines), axis), 0, {})
    for k, line in zip(turns, lines):
        slab = both[:, at : at + len(line)].reshape(len(both), -1)
        found[k] = slab[:, : leaves[k].size].reshape(-1, *leaves[k].shape)
        at += len(line)
    numbers = iter(range(len(leaves)))
    return jax.tree.map(lambda _: found[next(numbers)], x)


def prefix(value, axis, join, neutral):
    count, mine = (lax.axis_size(axis), lax.axis_index(axis))
    pieces = collected_together(value, axis)
    total = jax.tree.map(
        lambda part, zero: jnp.full_like(part, 0) + jnp.asarray(zero, part.dtype), value, neutral
    )

    def turn(position, total):
        longer = join(total, jax.tree.map(lambda part: part[position], pieces))
        return jax.tree.map(lambda new, old: jnp.where(position < mine, new, old), longer, total)

    return lax.fori_loop(0, count - 1, turn, total)


def sent_to_all(x, axis):
    copies = jnp.broadcast_to(x, (lax.axis_size(axis), *x.shape))
    return lax.all_to_all(copies, axis, split_axis=0, concat_axis=0, tiled=True)


def laid_out(parts, dim):
    lengths = list(parts.shape[1:])
    lengths[dim] *= parts.shape[0]
    return jnp.moveaxis(parts, 0, dim).reshape(lengths)


def gathered_copies(x, axis, dim):
    parts = sent_to_all(x, axis)
    return laid_out(parts, dim)


def with_halo(x, sides, width):
    for axis, dim in sides:
        devices, length = (lax.axis_size(axis), x.shape[dim])
        up = [(i, (i + 1) % devices) for i in range(devices - 1)]
        down = [(j, i) for i, j in up]
        last = lax.slice_in_dim(x, length - width, length, axis=dim)
        leading = lax.slice_in_dim(x, 0, width, axis=dim)
        before = lax.ppermute(last, axis, up)
        after = lax.ppermute(leading, axis, down)
        x = jnp.concatenate([before, x, after], axis=dim)
    return x


def feature(array):
    wide = array.astype(jnp.float32)
    return jnp.where(wide > 0, wide + 1.0, jnp.exp(jnp.minimum(wide, 0.0)))


def depthwise(padded, kernel):
    rows = padded.shape[1] - 2
    columns = padded.shape[2] - 2
    total = jnp.zeros(padded.shape[:1] + (rows, columns) + padded.shape[3:], jnp.float32)
    for row_off in range(3):
        for col_off in range(3):
            total = (
                total
                + padded[:, row_off : row_off + rows, col_off : col_off + columns].astype(
                    jnp.float32
                )
                * kernel[row_off, col_off]
            )
    return (total[..., 0, :] * jax.nn.silu(total[..., 1, :])).astype(jnp.bfloat16)


def add_pair(earlier, later):
    return (earlier[0] + later[0], earlier[1] + later[1])


def local(stream, query_tokens, key_tokens, value_tokens, out_weight, in_weight, conv_weight):
    frames_dev, rows_dev, columns, head_cols = query_tokens.shape
    heads = head_cols // HD
    count_tok = rows_dev * columns
    highest = lax.Precision.HIGHEST
    query_map = feature(query_tokens).reshape(frames_dev, count_tok, heads, HD)
    key_map = feature(key_tokens).reshape(frames_dev, count_tok, heads, HD)
    value_map = value_tokens.astype(jnp.float32).reshape(frames_dev, count_tok, heads, HD)
    states = jnp.einsum("fnha,fnhb->fahb", key_map, value_map, precision=highest).reshape(
        frames_dev, HD, head_cols
    )
    norms = jnp.sum(key_map, axis=1).reshape(frames_dev, 1, head_cols)
    states, norms = sent_together((states, norms), "height", 2, 1)
    states = jnp.cumsum(states, axis=0)
    norms = jnp.cumsum(norms, axis=0)
    before = prefix(
        (states[-1], norms[-1]),
        "tm",
        add_pair,
        (jnp.zeros_like(states[-1]), jnp.zeros_like(norms[-1])),
    )
    states = states + before[0]
    norms = norms + before[1]
    states, norms = (gathered_copies(states, "height", 2), gathered_copies(norms, "height", 2))
    numerator = jnp.einsum(
        "fnha,fahb->fnhb", query_map, states.reshape(frames_dev, HD, heads, HD), precision=highest
    )
    denominator = jnp.einsum(
        "fnha,fha->fnh", query_map, norms.reshape(frames_dev, heads, HD), precision=highest
    )
    attended = (
        (numerator / denominator[..., None])
        .reshape(frames_dev, rows_dev, columns, head_cols)
        .astype(jnp.bfloat16)
    )
    project = jnp.dot(
        attended.reshape(-1, head_cols), out_weight, preferred_element_type=jnp.float32
    )
    mixed = (stream.astype(jnp.float32) + project.reshape(stream.shape)).astype(jnp.bfloat16)
    expanded = jnp.einsum(
        "frwd,djc->frwjc",
        mixed,
        lax.all_gather(in_weight, "height", axis=2, tiled=True),
        preferred_element_type=jnp.float32,
    ).astype(jnp.bfloat16)
    padded = with_halo(expanded, (("height", 1),), 1)
    padded = jnp.pad(padded, ((0, 0), (0, 0), (1, 1), (0, 0), (0, 0)))
    gated = depthwise(padded, conv_weight)
    return (attended, gated)


def solution(mesh):
    placed = (
        P("tm", "height", None, None),
        P("tm", "height", None, None),
        P("tm", "height", None, None),
        P("tm", "height", None, None),
        P(),
        P(None, None, "height"),
        P(),
    )
    return jax.shard_map(
        local,
        mesh=mesh,
        in_specs=placed,
        out_specs=(P("tm", "height", None, None), P("tm", "height", None, None)),
        check_vma=False,
    )
```

profile of v0, /device:TPU:1, one launch (start us, length us, event | category | flops | bytes accessed | tf_op | source)
XLA Modules:
  0.0 300.8 jit_solution(4351893791225012609)
XLA Ops:
  7.2 0.7 all-gather.4.cloned.1.call-update
  7.9 2.2 fusion.25
  10.1 4.4 %reshape.183 = f32[640,10,112]{2,1,0:T(8,128)} reshape(f32[1,4,160,1120]{3,2,1,0:T(8,128)S(1)} %get-tuple-element.171) | data formatting | bytes 5734400 | tf_op jit(solution)/shard_map/reshape.1
  14.4 4.5 %reshape.184 = bf16[640,10,112]{2,1,0:T(8,128)(2,1)S(1)} reshape(bf16[1,4,160,1120]{3,2,1,0:T(8,128)(2,1)} %param.12) | data formatting | bytes 2867200 | tf_op jit(solution)/shard_map/reshape
  18.9 6.3 %fusion.32 = f32[1,112,10,112]{3,1,2,0:T(8,128)S(1)} fusion(bf16[640,10,112]{2,1,0:T(8,128)(2,1)S(1)} %reshape.184, f32[640,10,112]{2,1,0:T(8,128)} %reshape.183), kind=kOutput, calls=%fused_computation.47 | convolution fusion | flops 963379200 | bytes 4802560 | tf_op jit(solution)/shard_map/fnha,fnhb->fahb/dot_general | solution.py:121
  25.3 0.2 copy.54
  25.5 0.3 concatenate.27
  25.8 0.2 maximum_bitcast_fusion
  26.1 1.4 copy.56
  27.5 8.6 %all-to-all-start = ((f32[16,1,113,70]{2,1,3,0:T(1,128)}), f32[16,1,113,70]{2,1,3,0:T(1,128)S(1)}, u32[]{:S(2)}, u32[]{:S(2)}) async-start(f32[16,1,113,70]{2,1,3,0:T(1,128)} %copy.56), calls=%async_computation | async-start | bytes 1146880 | tf_op jit(solution)/shard_map/all_to_all | solution.py:17
  36.1 15.6 %all-to-all-done = f32[16,1,113,70]{2,1,3,0:T(1,128)S(1)} async-done(((f32[16,1,113,70]{2,1,3,0:T(1,128)}), f32[16,1,113,70]{2,1,3,0:T(1,128)S(1)}, u32[]{:S(2)}, u32[]{:S(2)}) %all-to-all-start) | async-done | bytes 506272 | tf_op jit(solution)/shard_map/all_to_all | solution.py:17
  51.7 0.5 reduce_sum.21
  52.4 15.6 %all-gather.1 = f32[8,113,70]{1,2,0:T(8,128)S(1)} all-gather(f32[1,113,70]{1,2,0:T(8,128)S(1)} %maximum_bitcast_fusion.1), channel_id=2, replica_groups=mesh['tm'=8,'height'=16] {'tm'}, dimensions={0}, use_global_device_ids=true | all-gather | bytes 284760 | tf_op jit(solution)/shard_map/all_gather | solution.py:36
  67.9 0.1 slice.99
  68.1 0.2 copy.60
  68.2 1.2 while.16
  68.2 0.1 copy.96
  68.4 0.1 copy.96
  68.6 0.1 copy.96
  68.8 0.1 copy.96
  69.5 0.1 copy.63
  69.6 0.2 add_reduce_fusion
  69.8 0.6 broadcast_in_dim.24
  70.4 5.5 %all-to-all-start.2 = ((f32[16,1,1,70]{3,2,1,0:T(1,128)}), f32[16,1,1,70]{3,2,1,0:T(1,128)S(1)}, u32[]{:S(2)}, u32[]{:S(2)}) async-start(f32[16,1,1,70]{3,2,1,0:T(1,128)} %broadcast_in_dim.24), calls=%async_computation.2 | async-start | bytes 16384 | tf_op jit(solution)/shard_map/all_to_all | solution.py:61
  76.0 6.4 %all-to-all-done.2 = f32[16,1,1,70]{3,2,1,0:T(1,128)S(1)} async-done(((f32[16,1,1,70]{3,2,1,0:T(1,128)}), f32[16,1,1,70]{3,2,1,0:T(1,128)S(1)}, u32[]{:S(2)}, u32[]{:S(2)}) %all-to-all-start.2) | async-done | bytes 4512 | tf_op jit(solution)/shard_map/all_to_all | solution.py:61
  82.4 1.1 broadcast_in_dim.22
  83.5 3.8 %all-to-all-start.1 = ((f32[16,1,112,70]{2,1,3,0:T(1,128)}), f32[16,1,112,70]{2,1,3,0:T(1,128)S(1)}, u32[]{:S(2)}, u32[]{:S(2)}) async-start(f32[16,1,112,70]{2,1,3,0:T(1,128)} %broadcast_in_dim.22), calls=%async_computation.1 | async-start | bytes 1146880 | tf_op jit(solution)/shard_map/all_to_all | solution.py:61
  87.3 2.0 fusion.27
  89.4 4.4 %reshape.185 = f32[640,10,112]{2,1,0:T(8,128)} reshape(f32[1,4,160,1120]{3,2,1,0:T(8,128)S(1)} %fusion.27) | data formatting | bytes 5734400 | tf_op jit(solution)/shard_map/reshape.7
  93.7 8.1 %copy.73 = f32[640,10,112]{0,2,1:T(8,128)S(1)} copy(f32[640,10,112]{2,1,0:T(8,128)} %reshape.185) | data formatting | bytes 5734400 | tf_op jit(solution)/shard_map/reshape.7
  101.9 0.5 broadcast.81
  102.4 0.7 reduce.8
  103.2 1.6 fusion.40
  104.8 3.5 %fusion.29 = bf16[1,640,10,112]{1,3,2,0:T(8,128)(2,1)} fusion(f32[112,10,112]{0,2,1:T(8,128)S(1)} %bitcast.141, f32[640,10,112]{0,2,1:T(8,128)S(1)} %copy.73, f32[640,10]{0,1:T(8,128)S(1)} %bitcast.142), kind=kOutput, calls=%fused_computation.44 | convolution fusion | flops 964812800 | bytes 4828160 | tf_op jit(solution)/shard_map/fnha,fahb->fnhb/dot_general | solution.py:137
  108.3 4.9 %convert_element_type.85 = bf16[4,160,1120]{1,0,2:T(4,128)(2,1)S(1)} reshape(bf16[1,640,10,112]{1,3,2,0:T(8,128)(2,1)} %fusion.29) | data formatting | bytes 2867200 | tf_op jit(solution)/shard_map/convert_element_type | solution.py:146
  113.3 8.5 %fusion.20 = bf16[4,160,2240,1]{2,1,3,0:T(8,128)(2,1)} fusion(bf16[1120,2240]{1,0:T(8,128)(2,1)} %param.13, bf16[1,4,160,2240]{3,2,1,0:T(8,128)(2,1)} %param.9, bf16[4,160,1120]{1,0,2:T(4,128)(2,1)S(1)} %convert_element_type.85), kind=kOutput, calls=%fused_computation.36 | convolution fusion | flops 3215564800 | bytes 12185600 | tf_op jit(solution)/shard_map/dot_general | solution.py:148
  121.8 61.3 %all-gather.4.cloned.1.call-done = bf16[2240,2,2800]{0,1,2:T(2,128)(2,1)} async-done(((bf16[2240,2,175]{0,1,2:T(2,128)(2,1)}), bf16[2240,2,2800]{0,1,2:T(2,128)(2,1)}) %all-gather.4.cloned.1.call-update) | async-done | bytes 25088016 | tf_op jit(solution)/shard_map/all_gather | solution.py:155
  183.1 25.4 %fusion.15 = bf16[4,160,2,2800]{3,1,2,0:T(8,128)(2,1)} fusion(bf16[4,160,2240,1]{2,1,3,0:T(8,128)(2,1)} %fusion.20, bf16[2240,2,2800]{0,1,2:T(2,128)(2,1)} %all-gather.4.cloned.1.call-done), kind=kOutput, calls=%fused_computation.26 | convolution fusion | flops 16059904000 | bytes 35123200 | tf_op jit(solution)/shard_map/frwd,djc->frwjc/dot_general | solution.py:152
  208.6 4.1 %fusion.39 = (bf16[1,1,160,2,2800]{4,2,3,1,0:T(8,128)(2,1)}, bf16[1,1,160,2,2800]{4,2,3,1,0:T(8,128)(2,1)}) fusion(bf16[1,4,160,2,2800]{4,2,3,1,0:T(8,128)(2,1)} %bitcast.133), kind=kLoop, calls=%fused_computation.66 | loop fusion | bytes 7168000 | tf_op jit(solution)/shard_map/slice | solution.py:80
  212.7 4.0 %collective-permute-start = (bf16[1,1,160,2,2800]{4,2,3,1,0:T(8,128)(2,1)}, bf16[1,1,160,2,2800]{4,2,3,1,0:T(8,128)(2,1)}, u32[]{:S(2)}, u32[]{:S(2)}) collective-permute-start(bf16[1,1,160,2,2800]{4,2,3,1,0:T(8,128)(2,1)} %get-tuple-element.169), channel_id=1, source_target_pairs={{0,1},{1,2},{2,3},{3,4},{4,5},{5,6},{6,7},{7,8},{8,9},{9,10},{10,1... | collective-permute-start | bytes 5376008 | tf_op jit(solution)/shard_map/ppermute | solution.py:82
  216.7 1.3 collective-permute-start.1
  218.0 5.2 %convert_element_type.83 = bf16[1,4,160,1120]{2,1,3,0:T(4,128)(2,1)S(1)} reshape(bf16[1,640,10,112]{1,3,2,0:T(8,128)(2,1)} %fusion.29) | data formatting | bytes 2867200 | tf_op jit(solution)/shard_map/convert_element_type | solution.py:146
  223.2 3.3 %copy.67 = bf16[1,4,160,1120]{3,2,1,0:T(8,128)(2,1)} copy(bf16[1,4,160,1120]{2,1,3,0:T(4,128)(2,1)S(1)} %convert_element_type.83) | data formatting | bytes 2867200
  226.6 27.0 %collective-permute-done = bf16[1,1,160,2,2800]{4,2,3,1,0:T(8,128)(2,1)} collective-permute-done((bf16[1,1,160,2,2800]{4,2,3,1,0:T(8,128)(2,1)}, bf16[1,1,160,2,2800]{4,2,3,1,0:T(8,128)(2,1)}, u32[]{:S(2)}, u32[]{:S(2)}) %collective-permute-start) | collective-permute-done | bytes 1792032 | tf_op jit(solution)/shard_map/ppermute | solution.py:82
  253.6 5.0 %collective-permute-done.1 = bf16[1,1,160,2,2800]{4,2,3,1,0:T(8,128)(2,1)} collective-permute-done((bf16[1,1,160,2,2800]{4,2,3,1,0:T(8,128)(2,1)}, bf16[1,1,160,2,2800]{4,2,3,1,0:T(8,128)(2,1)}, u32[]{:S(2)}, u32[]{:S(2)}) %collective-permute-start.1) | collective-permute-done | bytes 1792032 | tf_op jit(solution)/shard_map/ppermute | solution.py:83
  258.7 9.2 %fusion.12 = bf16[1,6,162,2,2800]{4,2,3,1,0:T(8,128)(2,1)S(1)} fusion(bf16[1,1,160,2,2800]{4,2,3,1,0:T(8,128)(2,1)} %collective-permute-done.1, bf16[1,4,160,2,2800]{4,2,3,1,0:T(8,128)(2,1)} %bitcast.134, bf16[1,1,160,2,2800]{4,2,3,1,0:T(8,128)(2,1)} %collective-permute-done), kind=kLoop, calls=%fused_computation.19 | loop fusion | flops 65318400 | bytes 21638400 | tf_op jit(solution)/shard_map/concatenate | solution.py:84
  267.9 18.5 %fusion.7 = f32[1,4,160,2,2800]{4,2,3,1,0:T(8,128)} fusion(bf16[4,160,2,2800]{3,1,2,0:T(8,128)(2,1)} %fusion.15, bf16[1,6,162,2,2800]{4,2,3,1,0:T(8,128)(2,1)S(1)} %fusion.12, bf16[1,1,160,2,2800]{4,2,3,1,0:T(8,128)(2,1)} %collective-permute-done.1, bf16[1,4,160,2,2800]{4,2,3,1,0:T(8,128)(2,1)} %bitcast.135, ...), kind=kLoop, calls=%fused_computation.14 | loop fusion | flops 100352000 | bytes 75465600 | tf_op jit(solution)/shard_map/add | solution.py:100
  286.4 7.5 %fusion.14 = bf16[1,4,160,2800]{3,2,1,0:T(8,128)(2,1)} fusion(f32[1,4,160,2,2800]{4,2,3,1,0:T(8,128)} %fusion.7), kind=kLoop, calls=%fused_computation.23 | loop fusion | flops 10752000 | bytes 17920000 | tf_op jit(solution)/shard_map/convert_element_type | solution.py:106
  (39 shorter events, 1.0 us)
Async XLA Ops:
  7.2 176.0 %all-gather.4.cloned.1.call-start = ((), (), s32[]{:S(2)}) async-start(), calls=%async_computation.3 | async-start | bytes 27417600 | tf_op jit(solution)/shard_map/all_gather | solution.py:155
  27.5 24.2 %all-to-all-start = ((f32[16,1,113,70]{2,1,3,0:T(1,128)}), f32[16,1,113,70]{2,1,3,0:T(1,128)S(1)}, u32[]{:S(2)}, u32[]{:S(2)}) async-start(f32[16,1,113,70]{2,1,3,0:T(1,128)} %copy.56), calls=%async_computation | async-start | bytes 1146880 | tf_op jit(solution)/shard_map/all_to_all | solution.py:17
  70.4 12.1 %all-to-all-start.2 = ((f32[16,1,1,70]{3,2,1,0:T(1,128)}), f32[16,1,1,70]{3,2,1,0:T(1,128)S(1)}, u32[]{:S(2)}, u32[]{:S(2)}) async-start(f32[16,1,1,70]{3,2,1,0:T(1,128)} %broadcast_in_dim.24), calls=%async_computation.2 | async-start | bytes 16384 | tf_op jit(solution)/shard_map/all_to_all | solution.py:61
  83.5 21.2 %all-to-all-start.1 = ((f32[16,1,112,70]{2,1,3,0:T(1,128)}), f32[16,1,112,70]{2,1,3,0:T(1,128)S(1)}, u32[]{:S(2)}, u32[]{:S(2)}) async-start(f32[16,1,112,70]{2,1,3,0:T(1,128)} %broadcast_in_dim.22), calls=%async_computation.1 | async-start | bytes 1146880 | tf_op jit(solution)/shard_map/all_to_all | solution.py:61
  208.6 9.4 %copy-start = (f32[3,3,2,2800]{3,2,1,0:T(2,128)S(1)}, f32[3,3,2,2800]{3,2,1,0:T(2,128)}, u32[]{:S(2)}) copy-start(f32[3,3,2,2800]{3,2,1,0:T(2,128)} %param.15) | copy-start | bytes 604804
  212.7 40.9 %collective-permute-start = (bf16[1,1,160,2,2800]{4,2,3,1,0:T(8,128)(2,1)}, bf16[1,1,160,2,2800]{4,2,3,1,0:T(8,128)(2,1)}, u32[]{:S(2)}, u32[]{:S(2)}) collective-permute-start(bf16[1,1,160,2,2800]{4,2,3,1,0:T(8,128)(2,1)} %get-tuple-element.169), channel_id=1, source_target_pairs={{0,1},{1,2},{2,3},{3,4},{4,5},{5,6},{6,7},{7,8},{8,9},{9,10},{10,1... | collective-permute-start | bytes 5376008 | tf_op jit(solution)/shard_map/ppermute | solution.py:82
  216.7 41.9 %collective-permute-start.1 = (bf16[1,1,160,2,2800]{4,2,3,1,0:T(8,128)(2,1)}, bf16[1,1,160,2,2800]{4,2,3,1,0:T(8,128)(2,1)}, u32[]{:S(2)}, u32[]{:S(2)}) collective-permute-start(bf16[1,1,160,2,2800]{4,2,3,1,0:T(8,128)(2,1)} %get-tuple-element.170), channel_id=1, source_target_pairs={{1,0},{2,1},{3,2},{4,3},{5,4},{6,5},{7,6},{8,7},{9,8},{10,9},{11,1... | collective-permute-start | bytes 5376008 | tf_op jit(solution)/shard_map/ppermute | solution.py:83
Sparse Core Ops, SparseCore 0:
  10.1 172.9 all-gather.3
where the time goes:
time: 302 us; the launch traced here: 301 us
  waiting for transfers between devices  116 us (38%)
  matrix products  45.4 us (15%)
  local copies, waits for them, and re-layouts  44.6 us (15%)
  other arithmetic  41.3 us (14%)
  starting transfers between devices  23.2 us (8%)
  blocking collectives  15.6 us (5%)
  between operations  14.2 us (5%)
    all_gather x1, waiting for transfers between devices, local(): lax.all_gather(in_weight, 'height', axis=2, tiled=True)  61.3 us
    ppermute x1, waiting for transfers between devices, with_halo(): before = lax.ppermute(last, axis, up)  27 us
    dot_general x1, matrix products, local(): jnp.einsum('frwd,djc->frwjc', mixed, lax.all_gather(in_weight, 'height',...  25.4 us
    add x1, other arithmetic, depthwise(): total + padded[:, row_off:row_off + rows, col_off:col_off + columns].asty...  18.5 us
    another operation x4, local copies, waits for them, and re-layouts  17 us
    all_gather x1, blocking collectives, collected_together(): both, at, found = (lax.all_gather(jnp.concatenate(lines), axis), 0, {})  15.6 us
    all_to_all x1, waiting for transfers between devices, sent_and_summed(): lax.all_to_all(parts, axis, split_axis=0, concat_axis=0, tiled=True)  15.6 us
    convert_element_type x2, local copies, waits for them, and re-layouts, local(): attended = (numerator / denominator[..., None]).reshape(frames_dev, rows_...  10.1 us
  transfers between devices with their start and end apart: 6, of which 5 were waited for; matrix products, arithmetic and copies ran while one was open for 22% of the time, Pallas kernels for 0%

commit v1 on v0

--- a/solution.py
+++ b/solution.py
@@ -1,6 +1,10 @@
+import functools
+
 import jax
 import jax.numpy as jnp
 from jax import lax
+from jax.experimental import pallas as pl
+from jax.experimental.pallas import tpu as pltpu
 from jax.sharding import PartitionSpec as P
 
 HD = 112
@@ -72,38 +76,68 @@
     return laid_out(parts, dim)
 
 
-def with_halo(x, sides, width):
-    for axis, dim in sides:
-        devices, length = (lax.axis_size(axis), x.shape[dim])
-        up = [(i, (i + 1) % devices) for i in range(devices - 1)]
-        down = [(j, i) for i, j in up]
-        last = lax.slice_in_dim(x, length - width, length, axis=dim)
-        leading = lax.slice_in_dim(x, 0, width, axis=dim)
-        before = lax.ppermute(last, axis, up)
-        after = lax.ppermute(leading, axis, down)
-        x = jnp.concatenate([before, x, after], axis=dim)
-    return x
-
-
 def feature(array):
     wide = array.astype(jnp.float32)
     return jnp.where(wide > 0, wide + 1.0, jnp.exp(jnp.minimum(wide, 0.0)))
 
 
-def depthwise(padded, kernel):
-    rows = padded.shape[1] - 2
-    columns = padded.shape[2] - 2
-    total = jnp.zeros(padded.shape[:1] + (rows, columns) + padded.shape[3:], jnp.float32)
-    for row_off in range(3):
-        for col_off in range(3):
-            total = (
-                total
-                + padded[:, row_off : row_off + rows, col_off : col_off + columns].astype(
-                    jnp.float32
-                )
-                * kernel[row_off, col_off]
-            )
-    return (total[..., 0, :] * jax.nn.silu(total[..., 1, :])).astype(jnp.bfloat16)
+def ffn_kernel(m_ref, wa_ref, wb_ref, cw_ref, o_ref, ev, eg):
+    nt = (((1,), (1,)), ((), ()))
+    for r0 in range(0, 6, 2):
+        rows = slice(r0 * 160, (r0 + 2) * 160)
+        acc = lax.dot_general(
+            m_ref[0, rows], wa_ref[...].reshape(256, 1152), nt, preferred_element_type=jnp.float32
+        )
+        acc = acc + lax.dot_general(
+            m_ref[1, rows], wb_ref[...].reshape(256, 1152), nt, preferred_element_type=jnp.float32
+        )
+        for r in range(2):
+            ev[r0 + r, 8:168] = acc[r * 160 : (r + 1) * 160, :128]
+            eg[r0 + r, 8:168] = acc[r * 160 : (r + 1) * 160, 128:]
+    zero = jnp.zeros((8, 128), jnp.float32)
+    for e in (ev, eg):
+        for r in range(6):
+            e[r, 0:8] = zero
+            e[r, 168:176] = zero
+    step = 16
+    taps = [
+        [jnp.broadcast_to(cw_ref[i * 2 + j : i * 2 + j + 1], (8, 128)) for i in range(9)]
+        for j in range(2)
+    ]
+    for k in range(0, 160, step):
+        sums = []
+        for e, w in ((ev, taps[0]), (eg, taps[1])):
+            acc = [None] * 4
+            for r in range(6):
+                for b in range(3):
+                    x = e[r, k + 7 + b : k + 7 + b + step].reshape(step // 8, 8, 128)
+                    for a in range(3):
+                        o = r - a
+                        if 0 <= o < 4:
+                            t = (x * w[a * 3 + b]).reshape(step, 128)
+                            acc[o] = t if acc[o] is None else acc[o] + t
+            sums.append(acc)
+        for o in range(4):
+            v, g = sums[0][o], sums[1][o]
+            res = (0.5 * v * g) * (1.0 + jnp.tanh(0.5 * g))
+            o_ref[o, k : k + step] = res.astype(jnp.bfloat16)
+
+
+def ffn(m, wa, wb, cw):
+    return pl.pallas_call(
+        ffn_kernel,
+        grid=(22,),
+        in_specs=[
+            pl.BlockSpec((2, 960, 1152), lambda b: (0, 0, 0)),
+            pl.BlockSpec((2, 128, 1152), lambda b: (0, b, 0)),
+            pl.BlockSpec((2, 128, 1152), lambda b: (0, b, 0)),
+            pl.BlockSpec((18, 128), lambda b: (0, b)),
+        ],
+        out_specs=pl.BlockSpec((4, 160, 128), lambda b: (0, 0, b)),
+        out_shape=jax.ShapeDtypeStruct((4, 160, 2800), jnp.bfloat16),
+        scratch_shapes=[pltpu.VMEM((6, 176, 128), jnp.float32)] * 2,
+        compiler_params=pltpu.CompilerParams(vmem_limit_bytes=40 * 2**20),
+    )(m, wa, wb, cw)
 
 
 def add_pair(earlier, later):
@@ -149,15 +183,23 @@
         attended.reshape(-1, head_cols), out_weight, preferred_element_type=jnp.float32
     )
     mixed = (stream.astype(jnp.float32) + project.reshape(stream.shape)).astype(jnp.bfloat16)
-    expanded = jnp.einsum(
-        "frwd,djc->frwjc",
-        mixed,
-        lax.all_gather(in_weight, "height", axis=2, tiled=True),
-        preferred_element_type=jnp.float32,
-    ).astype(jnp.bfloat16)
-    padded = with_halo(expanded, (("height", 1),), 1)
-    padded = jnp.pad(padded, ((0, 0), (0, 0), (1, 1), (0, 0), (0, 0)))
-    gated = depthwise(padded, conv_weight)
+    height, tm = lax.axis_index("height"), lax.axis_index("tm")
+    core = tm % 2
+    heights = lax.axis_size("height")
+    wt = jnp.pad(in_weight.transpose(2, 1, 0), ((0, 0), (0, 0), (0, 64)))
+    wt = lax.dynamic_slice(wt, (0, 0, core * 1152), (175, 2, 1152))
+    after = lax.ppermute(wt[:16], "height", [(i + 1, i) for i in range(heights - 1)])
+    wt = lax.dynamic_slice(jnp.concatenate([wt, after]), (height, 0, 0), (176, 2, 1152))
+    wa = lax.all_gather(wt.transpose(1, 0, 2), "height", axis=1, tiled=True)
+    wb = lax.ppermute(wa, "tm", [(i, i ^ 1) for i in range(8)])
+    mixed = mixed[0]
+    above = lax.ppermute(mixed[3:], "height", [(i, i + 1) for i in range(heights - 1)])
+    below = lax.ppermute(mixed[:1], "height", [(i + 1, i) for i in range(heights - 1)])
+    mixed = jnp.concatenate([above, mixed, below]).reshape(960, 2240)
+    mixed = jnp.pad(mixed, ((0, 0), (0, 64)))
+    mine = lax.dynamic_slice(mixed, (0, core * 1152), (960, 1152))
+    other = lax.dynamic_slice(mixed, (0, (1 - core) * 1152), (960, 1152))
+    gated = ffn(jnp.stack([mine, other]), wa, wb, conv_weight.reshape(18, 2800))[None]
     return (attended, gated)
 
 

time: 302 us -> 294 us (0.974)
  Pallas kernels: 0 us -> 40.4 us
  other arithmetic: 41.3 us -> 10.4 us
  matrix products: 45.4 us -> 18.7 us
  waiting for transfers between devices: 116 us -> 127 us
  starting transfers between devices: 23.2 us -> 19.1 us
    pallas_call x0 -> x1, Pallas kernels: none -> 40.4 us  [ffn(): pl.pallas_call(ffn_kernel, grid=(22,), in_specs=[pl.BlockSpec((2, 960, 11...]
    all_gather x1, waiting for transfers between devices: 61.3 us -> 97.4 us  [local(): wa = lax.all_gather(wt.transpose(1, 0, 2), 'height', axis=1, tiled=True)]
    dot_general x1 -> x0, matrix products: 25.4 us -> none  [local(): jnp.einsum('frwd,djc->frwjc', mixed, lax.all_gather(in_weight, 'height',...]
    ppermute x2 -> x4, waiting for transfers between devices: 32.1 us -> 12.9 us  [the longest x1 4.63 us: local(): lax.ppermute(wt[:16], 'height', [(i + 1, i) for i in range(heights - 1)])]
    add x1 -> x0, other arithmetic: 18.5 us -> none  [depthwise(): total + padded[:, row_off:row_off + rows, col_off:col_off + columns].asty...]
    convert_element_type x1 -> x0, other arithmetic: 7.46 us -> none  [depthwise(): (total[..., 0, :] * jax.nn.silu(total[..., 1, :])).astype(jnp.bfloat16)]
    concatenate x1, other arithmetic: 9.25 us -> 2.34 us  [local(): mixed = jnp.concatenate([above, mixed, below]).reshape(960, 2240)]
    all_to_all x1, waiting for transfers between devices: 15.6 us -> 10.5 us  [sent_and_summed(): lax.all_to_all(parts, axis, split_axis=0, concat_axis=0, tiled=True)]
  transfers between devices with their start and end apart: 6 -> 8, of which waited for: 5 -> 6; matrix products, arithmetic and copies ran while one was open for 22% -> 24% of each run, Pallas kernels for 0% -> 0%
where the time goes in v1:
time: 294 us; the launch traced here: 291 us
  waiting for transfers between devices  127 us (43%)
  local copies, waits for them, and re-layouts  45.6 us (16%)
  Pallas kernels  40.4 us (14%)
  starting transfers between devices  19.1 us (6%)
  matrix products  18.7 us (6%)
  blocking collectives  15.4 us (5%)
  between operations  14.3 us (5%)
  other arithmetic  10.4 us (4%)
    all_gather x1, waiting for transfers between devices, local(): wa = lax.all_gather(wt.transpose(1, 0, 2), 'height', axis=1, tiled=True)  97.4 us
    pallas_call x1, Pallas kernels, ffn(): pl.pallas_call(ffn_kernel, grid=(22,), in_specs=[pl.BlockSpec((2, 960, 11...  40.4 us
    another operation x4, local copies, waits for them, and re-layouts  16.9 us
    all_gather x1, blocking collectives, collected_together(): both, at, found = (lax.all_gather(jnp.concatenate(lines), axis), 0, {})  15.4 us
    all_to_all x1, waiting for transfers between devices, sent_and_summed(): lax.all_to_all(parts, axis, split_axis=0, concat_axis=0, tiled=True)  10.5 us
    convert_element_type x2, local copies, waits for them, and re-layouts, local(): attended = (numerator / denominator[..., None]).reshape(frames_dev, rows_...  9.86 us
    all_to_all x2, starting transfers between devices, sent_to_all(): return lax.all_to_all(copies, axis, split_axis=0, concat_axis=0, tiled=True)  7.23 us
    dot_general x1, matrix products, local(): jnp.dot(attended.reshape(-1, head_cols), out_weight, preferred_element_ty...  7.22 us
  transfers between devices with their start and end apart: 8, of which 6 were waited for; matrix products, arithmetic and copies ran while one was open for 24% of the time, Pallas kernels for 0%

profile of v1, /device:TPU:1, one launch (start us, length us, event | category | flops | bytes accessed | tf_op | source)
XLA Modules:
  0.0 291.2 jit_solution(12235969855529051967)
XLA Ops:
  7.2 1.6 copy.82
  8.8 1.3 collective-permute-start.2
  10.2 0.2 pad_dynamic-slice_fusion.3
  10.3 4.6 %collective-permute-done.2 = bf16[16,2,1152]{2,0,1:T(8,128)(2,1)S(1)} collective-permute-done((bf16[16,2,1152]{2,0,1:T(8,128)(2,1)S(1)}, bf16[16,2,1152]{2,0,1:T(8,128)(2,1)S(1)}, u32[]{:S(2)}, u32[]{:S(2)}) %collective-permute-start.2) | collective-permute-done | bytes 73760 | tf_op jit(solution)/shard_map/ppermute | solution.py:191
  14.9 1.6 fusion.19
  16.5 97.4 %all-gather.4.cloned.1.call-done.wa_ref = bf16[2,2816,1152]{2,1,0:T(8,128)(2,1)} async-done(((bf16[2,176,1152]{2,1,0:T(8,128)(2,1)}), bf16[2,2816,1152]{2,1,0:T(8,128)(2,1)}) %all-gather.4.cloned.1.call-update) | async-done | bytes 12976144 | tf_op jit(solution)/shard_map/all_gather | solution.py:193
  113.9 0.8 collective-permute-start.3
  114.7 2.2 fusion.4
  116.9 4.4 %reshape.104 = f32[640,10,112]{2,1,0:T(8,128)} reshape(f32[1,4,160,1120]{3,2,1,0:T(8,128)S(1)} %get-tuple-element.173) | data formatting | bytes 5734400 | tf_op jit(solution)/shard_map/reshape.1
  121.3 4.5 %reshape.105 = bf16[640,10,112]{2,1,0:T(8,128)(2,1)S(1)} reshape(bf16[1,4,160,1120]{3,2,1,0:T(8,128)(2,1)} %param.12) | data formatting | bytes 2867200 | tf_op jit(solution)/shard_map/reshape
  125.8 6.3 %fusion.13 = f32[1,112,10,112]{3,1,2,0:T(8,128)S(1)} fusion(bf16[640,10,112]{2,1,0:T(8,128)(2,1)S(1)} %reshape.105, f32[640,10,112]{2,1,0:T(8,128)} %reshape.104), kind=kOutput, calls=%fused_computation.32 | convolution fusion | flops 963379200 | bytes 4802560 | tf_op jit(solution)/shard_map/fnha,fnhb->fahb/dot_general | solution.py:155
  132.1 0.2 copy.50
  132.3 0.3 concatenate.23
  132.7 0.2 maximum_bitcast_fusion
  132.9 1.4 copy.52
  134.3 5.0 %all-to-all-start = ((f32[16,1,113,70]{2,1,3,0:T(1,128)}), f32[16,1,113,70]{2,1,3,0:T(1,128)S(1)}, u32[]{:S(2)}, u32[]{:S(2)}) async-start(f32[16,1,113,70]{2,1,3,0:T(1,128)} %copy.52), calls=%async_computation | async-start | bytes 1146880 | tf_op jit(solution)/shard_map/all_to_all | solution.py:21
  139.3 10.5 %all-to-all-done = f32[16,1,113,70]{2,1,3,0:T(1,128)S(1)} async-done(((f32[16,1,113,70]{2,1,3,0:T(1,128)}), f32[16,1,113,70]{2,1,3,0:T(1,128)S(1)}, u32[]{:S(2)}, u32[]{:S(2)}) %all-to-all-start) | async-done | bytes 506272 | tf_op jit(solution)/shard_map/all_to_all | solution.py:21
  149.8 0.5 reduce_sum.21
  150.5 15.4 %all-gather.1 = f32[8,113,70]{1,2,0:T(8,128)S(1)} all-gather(f32[1,113,70]{1,2,0:T(8,128)S(1)} %maximum_bitcast_fusion.1), channel_id=2, replica_groups=mesh['tm'=8,'height'=16] {'tm'}, dimensions={0}, use_global_device_ids=true | all-gather | bytes 284760 | tf_op jit(solution)/shard_map/all_gather | solution.py:40
  166.1 0.2 copy.56
  166.2 1.2 while.16
  167.6 0.2 add_reduce_fusion
  167.8 0.6 broadcast_in_dim.27
  168.4 3.7 %all-to-all-start.2 = ((f32[16,1,1,70]{3,2,1,0:T(1,128)}), f32[16,1,1,70]{3,2,1,0:T(1,128)S(1)}, u32[]{:S(2)}, u32[]{:S(2)}) async-start(f32[16,1,1,70]{3,2,1,0:T(1,128)} %broadcast_in_dim.27), calls=%async_computation.2 | async-start | bytes 16384 | tf_op jit(solution)/shard_map/all_to_all | solution.py:65
  172.1 6.0 %all-to-all-done.2 = f32[16,1,1,70]{3,2,1,0:T(1,128)S(1)} async-done(((f32[16,1,1,70]{3,2,1,0:T(1,128)}), f32[16,1,1,70]{3,2,1,0:T(1,128)S(1)}, u32[]{:S(2)}, u32[]{:S(2)}) %all-to-all-start.2) | async-done | bytes 4512 | tf_op jit(solution)/shard_map/all_to_all | solution.py:65
  178.2 1.1 broadcast_in_dim.25
  179.3 3.6 %all-to-all-start.1 = ((f32[16,1,112,70]{2,1,3,0:T(1,128)}), f32[16,1,112,70]{2,1,3,0:T(1,128)S(1)}, u32[]{:S(2)}, u32[]{:S(2)}) async-start(f32[16,1,112,70]{2,1,3,0:T(1,128)} %broadcast_in_dim.25), calls=%async_computation.1 | async-start | bytes 1146880 | tf_op jit(solution)/shard_map/all_to_all | solution.py:65
  182.9 2.0 fusion.6
  184.9 4.4 %reshape.106 = f32[640,10,112]{2,1,0:T(8,128)} reshape(f32[1,4,160,1120]{3,2,1,0:T(8,128)S(1)} %fusion.6) | data formatting | bytes 5734400 | tf_op jit(solution)/shard_map/reshape.7
  189.3 8.1 %copy.67 = f32[640,10,112]{0,2,1:T(8,128)S(1)} copy(f32[640,10,112]{2,1,0:T(8,128)} %reshape.106) | data formatting | bytes 5734400 | tf_op jit(solution)/shard_map/reshape.7
  197.4 0.5 broadcast.44
  197.9 0.7 reduce.8
  198.6 1.6 fusion.22
  200.3 3.5 %fusion.8 = bf16[1,640,10,112]{1,3,2,0:T(8,128)(2,1)} fusion(f32[112,10,112]{0,2,1:T(8,128)S(1)} %bitcast.103, f32[640,10,112]{0,2,1:T(8,128)S(1)} %copy.67, f32[640,10]{0,1:T(8,128)S(1)} %bitcast.104), kind=kOutput, calls=%fused_computation.24 | convolution fusion | flops 964812800 | bytes 4828160 | tf_op jit(solution)/shard_map/fnha,fahb->fnhb/dot_general | solution.py:171
  203.8 4.9 %convert_element_type.42 = bf16[4,160,1120]{1,0,2:T(4,128)(2,1)S(1)} reshape(bf16[1,640,10,112]{1,3,2,0:T(8,128)(2,1)} %fusion.8) | data formatting | bytes 2867200 | tf_op jit(solution)/shard_map/convert_element_type | solution.py:180
  208.7 7.2 %fusion = bf16[1,4,160,2240]{3,2,1,0:T(8,128)(2,1)S(1)} fusion(bf16[1,4,160,2240]{3,2,1,0:T(8,128)(2,1)} %param.9, bf16[1120,2240]{1,0:T(8,128)(2,1)} %param.13, bf16[4,160,1120]{1,0,2:T(4,128)(2,1)S(1)} %convert_element_type.42), kind=kOutput, calls=%fused_computation.5 | convolution fusion | flops 3215564800 | bytes 12185600 | tf_op jit(solution)/shard_map/dot_general | solution.py:182
  216.0 1.6 copy-done
  217.6 1.2 slice_bitcast_fusion.1
  218.8 3.2 %collective-permute-start = (bf16[1,160,2240]{2,1,0:T(8,128)(2,1)}, bf16[1,160,2240]{2,1,0:T(8,128)(2,1)S(1)}, u32[]{:S(2)}, u32[]{:S(2)}) collective-permute-start(bf16[1,160,2240]{2,1,0:T(8,128)(2,1)} %get-tuple-element.171), channel_id=1, source_target_pairs={{0,1},{1,2},{2,3},{3,4},{4,5},{5,6},{6,7},{7,8},{8,9},{9,10},{10,1... | collective-permute-start | bytes 2150408 | tf_op jit(solution)/shard_map/ppermute | solution.py:196
  222.0 1.5 collective-permute-start.1
  223.6 4.9 %convert_element_type.40 = bf16[1,4,160,1120]{2,1,3,0:T(4,128)(2,1)S(1)} reshape(bf16[1,640,10,112]{1,3,2,0:T(8,128)(2,1)} %fusion.8) | data formatting | bytes 2867200 | tf_op jit(solution)/shard_map/convert_element_type | solution.py:180
  228.6 3.3 %copy.62 = bf16[1,4,160,1120]{3,2,1,0:T(8,128)(2,1)} copy(bf16[1,4,160,1120]{2,1,3,0:T(4,128)(2,1)S(1)} %convert_element_type.40) | data formatting | bytes 2867200
  231.9 4.4 %collective-permute-done = bf16[1,160,2240]{2,1,0:T(8,128)(2,1)S(1)} collective-permute-done((bf16[1,160,2240]{2,1,0:T(8,128)(2,1)}, bf16[1,160,2240]{2,1,0:T(8,128)(2,1)S(1)}, u32[]{:S(2)}, u32[]{:S(2)}) %collective-permute-start) | collective-permute-done | bytes 716832 | tf_op jit(solution)/shard_map/ppermute | solution.py:196
  236.3 3.9 %collective-permute-done.1 = bf16[1,160,2240]{2,1,0:T(8,128)(2,1)} collective-permute-done((bf16[1,160,2240]{2,1,0:T(8,128)(2,1)}, bf16[1,160,2240]{2,1,0:T(8,128)(2,1)}, u32[]{:S(2)}, u32[]{:S(2)}) %collective-permute-start.1) | collective-permute-done | bytes 716832 | tf_op jit(solution)/shard_map/ppermute | solution.py:197
  240.2 2.3 pad_maximum_fusion
  242.5 0.9 fusion.10
  243.4 0.4 pad_maximum_fusion.1.m_ref
  243.9 40.4 %shard_map.86 = bf16[4,160,2800]{2,1,0:T(8,128)(2,1)} custom-call(bf16[2,960,1152]{2,1,0:T(8,128)(2,1)S(1)} %pad_maximum_fusion.1.m_ref, bf16[2,2816,1152]{2,1,0:T(8,128)(2,1)} %all-gather.4.cloned.1.call-done.wa_ref, bf16[2,2816,1152]{2,1,0:T(8,128)(2,1)} %collective-permute-done.3.wb_ref, f32[18,2800]{1,0:T(8,128)S(1)} %reshape.96.cw_ref), custom_call_target="tpu_custom_call" | custom-call | tf_op jit(solution)/shard_map/pallas_call | solution.py:127
  (49 shorter events, 1.8 us)
Async XLA Ops:
  7.2 106.7 %all-gather.4.cloned.1.call-start = ((), (), s32[]{:S(2)}) async-start(), calls=%async_computation.3 | async-start | bytes 13787136 | tf_op jit(solution)/shard_map/all_gather | solution.py:193
  8.8 6.1 %collective-permute-start.2 = (bf16[16,2,1152]{2,0,1:T(8,128)(2,1)S(1)}, bf16[16,2,1152]{2,0,1:T(8,128)(2,1)S(1)}, u32[]{:S(2)}, u32[]{:S(2)}) collective-permute-start(bf16[16,2,1152]{2,0,1:T(8,128)(2,1)S(1)} %pad_dynamic-slice_fusion.2), channel_id=1, source_target_pairs={{1,0},{2,1},{3,2},{4,3},{5,4},{6,5},{7,6},{8,7},{9,8},{10,9},{11,1... | collective-permute-start | bytes 221192 | tf_op jit(solution)/shard_map/ppermute | solution.py:191
  113.9 130.0 %collective-permute-start.3 = (bf16[2,2816,1152]{2,1,0:T(8,128)(2,1)}, bf16[2,2816,1152]{2,1,0:T(8,128)(2,1)}, u32[]{:S(2)}, u32[]{:S(2)}) collective-permute-start(bf16[2,2816,1152]{2,1,0:T(8,128)(2,1)} %all-gather.4.cloned.1.call-done.wa_ref), channel_id=1, source_target_pairs={{0,16},{16,0},{32,48},{48,32},{64,80},{80,64},{96,112},{112,96},{1... | collective-permute-start | bytes 38928392 | tf_op jit(solution)/shard_map/ppermute | solution.py:194
  134.3 15.5 %all-to-all-start = ((f32[16,1,113,70]{2,1,3,0:T(1,128)}), f32[16,1,113,70]{2,1,3,0:T(1,128)S(1)}, u32[]{:S(2)}, u32[]{:S(2)}) async-start(f32[16,1,113,70]{2,1,3,0:T(1,128)} %copy.52), calls=%async_computation | async-start | bytes 1146880 | tf_op jit(solution)/shard_map/all_to_all | solution.py:21
  168.4 9.8 %all-to-all-start.2 = ((f32[16,1,1,70]{3,2,1,0:T(1,128)}), f32[16,1,1,70]{3,2,1,0:T(1,128)S(1)}, u32[]{:S(2)}, u32[]{:S(2)}) async-start(f32[16,1,1,70]{3,2,1,0:T(1,128)} %broadcast_in_dim.27), calls=%async_computation.2 | async-start | bytes 16384 | tf_op jit(solution)/shard_map/all_to_all | solution.py:65
  179.3 21.0 %all-to-all-start.1 = ((f32[16,1,112,70]{2,1,3,0:T(1,128)}), f32[16,1,112,70]{2,1,3,0:T(1,128)S(1)}, u32[]{:S(2)}, u32[]{:S(2)}) async-start(f32[16,1,112,70]{2,1,3,0:T(1,128)} %broadcast_in_dim.25), calls=%async_computation.1 | async-start | bytes 1146880 | tf_op jit(solution)/shard_map/all_to_all | solution.py:65
  216.0 1.6 copy-start
  217.6 5.9 %copy-start.1 = (f32[3,3,2,2800]{3,2,1,0:T(2,128)S(1)}, f32[3,3,2,2800]{3,2,1,0:T(2,128)}, u32[]{:S(2)}) copy-start(f32[3,3,2,2800]{3,2,1,0:T(2,128)} %param.15) | copy-start | bytes 604804
  218.8 17.5 %collective-permute-start = (bf16[1,160,2240]{2,1,0:T(8,128)(2,1)}, bf16[1,160,2240]{2,1,0:T(8,128)(2,1)S(1)}, u32[]{:S(2)}, u32[]{:S(2)}) collective-permute-start(bf16[1,160,2240]{2,1,0:T(8,128)(2,1)} %get-tuple-element.171), channel_id=1, source_target_pairs={{0,1},{1,2},{2,3},{3,4},{4,5},{5,6},{6,7},{7,8},{8,9},{9,10},{10,1... | collective-permute-start | bytes 2150408 | tf_op jit(solution)/shard_map/ppermute | solution.py:196
  222.0 18.2 %collective-permute-start.1 = (bf16[1,160,2240]{2,1,0:T(8,128)(2,1)}, bf16[1,160,2240]{2,1,0:T(8,128)(2,1)}, u32[]{:S(2)}, u32[]{:S(2)}) collective-permute-start(bf16[1,160,2240]{2,1,0:T(8,128)(2,1)} %get-tuple-element.172), channel_id=1, source_target_pairs={{1,0},{2,1},{3,2},{4,3},{5,4},{6,5},{7,6},{8,7},{9,8},{10,9},{11,1... | collective-permute-start | bytes 2150408 | tf_op jit(solution)/shard_map/ppermute | solution.py:197
Sparse Core Ops, SparseCore 0:
  16.6 97.1 all-gather.3

commit v2 on v0

v2 whole, which is shorter than its diff:
```python
import functools

import jax
import jax.numpy as jnp
from jax import lax
from jax.experimental import pallas as pl
from jax.experimental.pallas import tpu as pltpu
from jax.sharding import PartitionSpec as P

MESH = pl.DeviceIdType.MESH
F32, BF16 = jnp.float32, jnp.bfloat16
HD, TOK, COLS = 112, 640, 1120
SHARD, KH, CH = 176, 1152, 2816
TILES = (
    (0, 256, 0, 384),
    (256, 512, 128, 640),
    (512, 768, 384, 896),
    (768, 1024, 640, 1120),
    (1024, 1120, 896, 1120),
)


def phi(x):
    wide = x.astype(F32)
    return jnp.where(wide > 0, wide + 1.0, jnp.exp(jnp.minimum(wide, 0.0)))


def heads_of(t0, t1):
    return range(t0 // HD, (t1 - 1) // HD + 1)


def lanes_in(head, t0, t1):
    lanes = t0 + lax.broadcasted_iota(jnp.int32, (HD, t1 - t0), 1)
    return (lanes >= head * HD) & (lanes < (head + 1) * HD)


def kernel(
    q_h, k_h, v_h, s_h, ow_h, wp, cw,
    att_out, gated_out, w_all,
    q6, s6, kk, vv, ow, att, mix, own, got, tot, early, full, bd, hd, ev, eg, wbuf, obuf,
    load_sem, halo_s, halo_r, rs_s, rs_r, pre_s, pre_r, ag_s, ag_r,
    ring_s, y_s, dr_s, dy_s, ring_r, y_r, dr_r, dy_r, fill_sem, wb_sem, ob_sem, att_sem,
):
    tm, h = lax.axis_index("tm"), lax.axis_index("height")
    y, c = tm // 2, lax.rem(tm, 2)
    x, z = h // 4, lax.rem(h, 4)
    j0 = lax.rem(y, 2)
    j1 = 1 - j0

    loads = [
        pltpu.make_async_copy(k_h, kk, load_sem.at[0]),
        pltpu.make_async_copy(v_h, vv, load_sem.at[1]),
        pltpu.make_async_copy(q_h, q6.at[160:800], load_sem.at[2]),
        pltpu.make_async_copy(s_h, s6.at[160:800], load_sem.at[3]),
        pltpu.make_async_copy(ow_h, ow, load_sem.at[4]),
    ]
    fill = pltpu.make_async_copy(wp, w_all.at[:, :, pl.ds(pl.multiple_of(h * SHARD, 16), SHARD)], fill_sem)

    barrier = pltpu.get_barrier_semaphore()

    def greet(d, _):
        pl.semaphore_signal(barrier, inc=1, device_id={"tm": tm, "height": lax.rem(h + d, 16)}, device_id_type=MESH)
        return 0

    def greet_tm(d, _):
        pl.semaphore_signal(barrier, inc=1, device_id={"tm": lax.rem(tm + d, 8), "height": h}, device_id_type=MESH)
        return 0

    lax.fori_loop(1, 16, greet, 0)
    lax.fori_loop(1, 8, greet_tm, 0)
    for copy in loads:
        copy.start()
    fill.start()
    pl.semaphore_wait(barrier, 22)

    def send(src, dst, ssem, rsem, to_tm, to_h):
        return pltpu.make_async_remote_copy(
            src_ref=src, dst_ref=dst, send_sem=ssem, recv_sem=rsem,
            device_id={"tm": to_tm, "height": to_h}, device_id_type=MESH,
        )

    def at(dx, zz):
        return lax.rem(x + dx + 4, 4) * 4 + zz

    def zat(dz):
        return lax.rem(z + dz + 4, 4)

    def piece(o, kh, j):
        return w_all.at[kh, j, pl.ds(pl.multiple_of(o * SHARD, 16), SHARD)]

    def ring_send(o, to_h, src=None):
        dst = piece(o, c, j0)
        send(dst if src is None else src, dst, ring_s, ring_r.at[o], tm, to_h).start()

    def ring_wait(o):
        send(piece(o, c, j0), piece(o, c, j0), ring_s, ring_r.at[o], tm, h).wait_recv()

    def pass_on(o):
        low = lax.rem(o, 4) // 2
        yt = lax.rem(y + 3 + 2 * low, 4)
        p = piece(o, c, j0)
        send(p, p, y_s, y_r.at[o], yt * 2 + c, h).start()
        send(p, p, dr_s, dr_r.at[o], y * 2 + 1 - c, h).start()

    def y_take(o):
        p = piece(o, c, j1)
        send(p, p, y_s, y_r.at[o], tm, h).wait_recv()
        send(p, p, dy_s, dy_r.at[o], y * 2 + 1 - c, h).start()

    def d_wait(o):
        p = piece(o, 1 - c, j0)
        send(p, p, dr_s, dr_r.at[o], tm, h).wait_recv()
        p = piece(o, 1 - c, j1)
        send(p, p, dy_s, dy_r.at[o], tm, h).wait_recv()

    def to_x(o, src=None):
        ring_send(o, at(1, z), src)
        ring_send(o, at(-1, z), src)

    mine = wp.at[c, j0]
    dz = 1 - 2 * c
    ring_send(h, x * 4 + zat(1), mine)
    ring_send(h, x * 4 + zat(-1), mine)
    to_x(h, mine)

    own[...] = jnp.zeros(own.shape, F32)
    loads[0].wait()
    for r in range(0, TOK, 160):
        kk[r : r + 160] = phi(kk[r : r + 160]).astype(BF16)
    loads[1].wait()
    norm = jnp.sum(kk[...].astype(F32), axis=0, keepdims=True)
    own[14, :, :COLS] = jnp.broadcast_to(norm, (8, COLS))
    for t0, t1, w0, w1 in TILES:
        part = lax.dot_general(
            kk[:, w0:w1], vv[:, t0:t1], (((0,), (0,)), ((), ())), preferred_element_type=F32
        )
        state = jnp.zeros((HD, t1 - t0), F32)
        for head in heads_of(t0, t1):
            a = head * HD - w0
            state = jnp.where(lanes_in(head, t0, t1), part[a : a + HD], state)
        own[0:14, :, t0:t1] = state.reshape(14, 8, t1 - t0)

    def rs(d, _):
        to = lax.rem(h + d, 16)
        send(own.at[to], got.at[d - 1], rs_s, rs_r, tm, to).start()
        return 0

    lax.fori_loop(1, 16, rs, 0)

    zm, zp, zf = x * 4 + zat(-1), x * 4 + zat(1), x * 4 + zat(2)
    ring_wait(zm)
    ring_wait(zp)
    ring_send(x * 4 + zat(-dz), x * 4 + zat(dz))
    to_x(zm)

    loads[2].wait()
    for r in range(160, 800, 160):
        q6[r : r + 160] = phi(q6[r : r + 160]).astype(BF16)

    send(got, got, rs_s, rs_r, tm, h).wait_recv()
    tot[...] = own[h] + jnp.sum(got[...], axis=0)

    def pre(d, _):
        send(tot, early.at[d - 1], pre_s, pre_r, lax.rem(tm + d, 8), h).start()
        return 0

    lax.fori_loop(1, 8, pre, 0)
    to_x(zp)
    pass_on(zm)
    pass_on(zp)
    send(early, early, pre_s, pre_r, tm, h).wait_recv()
    causal = tot[...]
    for d in range(1, 8):
        causal = causal + jnp.where(d <= tm, early[d - 1], 0.0)
    full[h] = causal

    def ag(d, _):
        to = lax.rem(h + d, 16)
        send(full.at[h], full.at[h], ag_s, ag_r, tm, to).start()
        return 0

    lax.fori_loop(1, 16, ag, 0)

    up, down = lax.rem(h + 15, 16), lax.rem(h + 1, 16)
    halos = [
        send(q_h.at[480:640], q6.at[0:160], halo_s.at[0], halo_r.at[0], tm, down),
        send(q_h.at[0:160], q6.at[800:960], halo_s.at[1], halo_r.at[1], tm, up),
        send(s_h.at[480:640], s6.at[0:160], halo_s.at[2], halo_r.at[2], tm, down),
        send(s_h.at[0:160], s6.at[800:960], halo_s.at[3], halo_r.at[3], tm, up),
    ]
    for copy in halos:
        copy.start()

    ring_wait(zf)
    to_x(zf)
    pass_on(zf)

    def x_event(k):
        zz = zat(k)
        d = 1 - 2 * (zz // 2)
        ring_wait(at(-1, zz))
        ring_wait(at(1, zz))
        ring_send(lax.rem(x - d + 4, 4) * 4 + zz, lax.rem(x + d + 4, 4) * 4 + z)
        pass_on(at(-1, zz))
        pass_on(at(1, zz))

    def far_event(k):
        ring_wait(at(2, zat(k)))
        pass_on(at(2, zat(k)))

    x_event(0)

    send(full.at[0:15], full.at[0:15], ag_s, ag_r, tm, h).wait_recv()
    for i, (t0, t1, w0, w1) in enumerate(TILES):
        bd[i] = jnp.zeros(bd.shape[1:], BF16)
        hd[i] = jnp.zeros(hd.shape[1:], BF16)
        state = full[0:14, :, t0:t1].reshape(HD, t1 - t0)
        for head in heads_of(t0, t1):
            a, inside = head * HD - w0, lanes_in(head, t0, t1)
            bd[i, a : a + HD, : t1 - t0] = jnp.where(inside, state, 0.0).astype(BF16)
            hd[i, a : a + HD, : t1 - t0] = jnp.where(inside, 1.0, 0.0).astype(BF16)
    norms = full[14, 0:1, :COLS]

    def attend(r0, n):
        for i, (t0, t1, w0, w1) in enumerate(TILES):
            qw = q6[r0 : r0 + n, w0:w1]
            b, e = bd[i, : w1 - w0, : t1 - t0], hd[i, : w1 - w0, : t1 - t0]
            qn = qw.astype(F32) * norms[:, w0:w1]
            qa = qn.astype(BF16)
            qb = (qn - qa.astype(F32)).astype(BF16)
            num = jnp.dot(qw, b, preferred_element_type=F32)
            den = jnp.dot(qa, e, preferred_element_type=F32) + jnp.dot(qb, e, preferred_element_type=F32)
            att[r0 : r0 + n, t0:t1] = (num / den).astype(BF16)

    def project(r0, n, keep=None):
        for kh in range(2):
            for a in range(0, KH, 256):
                b = min(a + 256, KH if kh == 0 else 1088)
                cols = slice(kh * KH + a, kh * KH + b)
                p = jnp.dot(att[r0 : r0 + n], ow[:, cols], preferred_element_type=F32)
                p = p + s6[r0 : r0 + n, cols].astype(F32)
                if keep is not None:
                    p = jnp.where(keep, p, 0.0)
                mix[kh, r0 : r0 + n, a:b] = p.astype(BF16)
        mix[1, r0 : r0 + n, 1088:KH] = jnp.zeros((n, KH - 1088), BF16)

    attend(160, 640)
    out_copy = pltpu.make_async_copy(att.at[160:800], att_out, att_sem)
    out_copy.start()
    x_event(-1)
    x_event(1)
    y_take(zm)
    y_take(zp)
    loads[3].wait()
    loads[4].wait()
    project(160, 640)
    y_take(zf)
    x_event(2)
    for copy in halos:
        copy.wait_recv()
    for r, keep in ((0, h > 0), (800, h < 15)):
        q6[r : r + 160] = phi(q6[r : r + 160]).astype(BF16)
        attend(r, 160)
        project(r, 160, keep)

    def block_of(s):
        g = s // 5
        off = jnp.where(g == 2, 3, jnp.where(g == 3, 2, g))
        gx = lax.rem(x + off, 4)
        inner = 11 * (gx // 2) + 6 * lax.rem(gx, 2) + lax.rem(s, 5)
        return jnp.where(s < 20, inner, jnp.where(s == 20, 5, 16))

    def fetch(s):
        b = block_of(s)
        return pltpu.make_async_copy(
            w_all.at[:, :, pl.ds(pl.multiple_of(b * 128, 128), 128)], wbuf.at[lax.rem(s, 2)], wb_sem.at[lax.rem(s, 2)]
        )

    def put(s):
        b = block_of(s)
        return pltpu.make_async_copy(
            obuf.at[lax.rem(s, 2)], gated_out.at[:, :, pl.ds(pl.multiple_of(b * 128, 128), 128)], ob_sem.at[lax.rem(s, 2)]
        )

    zero = jnp.zeros((8, 128), F32)
    for e in (ev, eg):
        for r in range(6):
            e[r, 0:8] = zero
            e[r, 168:176] = zero
    fill.wait()
    d_wait(zm)
    d_wait(zp)
    d_wait(zf)
    fetch(0).start()
    nt = (((1,), (1,)), ((), ()))

    def ready(dx):
        for k in range(4):
            d_wait(at(dx, zat(k)))

    def at_step(s):
        if s == 0:
            y_take(at(-1, z)), y_take(at(1, z)), far_event(0)
        elif s == 1:
            y_take(at(-1, zat(-1))), y_take(at(1, zat(-1)))
        elif s == 2:
            y_take(at(-1, zat(1))), y_take(at(1, zat(1))), far_event(-1)
        elif s == 3:
            y_take(at(-1, zat(2))), y_take(at(1, zat(2))), far_event(1)
        elif s == 4:
            ready(1)
        elif s == 6:
            far_event(2)
        elif s == 8:
            y_take(at(2, z)), y_take(at(2, zat(-1)))
        elif s == 9:
            ready(-1)
        elif s == 12:
            y_take(at(2, zat(1))), y_take(at(2, zat(2)))
        elif s == 14:
            ready(2)

    events = (0, 1, 2, 3, 4, 6, 8, 9, 12, 14)

    def block(s, _):
        for e in events:
            pl.when(s == e)(functools.partial(at_step, e))
        slot = lax.rem(s, 2)

        @pl.when(s < 21)
        def _():
            fetch(s + 1).start()

        fetch(s).wait()
        b = block_of(s)
        for r0 in range(0, 6, 2):
            acc = None
            for kh in range(2):
                w = wbuf[slot, kh].reshape(256, KH)
                t = lax.dot_general(mix[kh, r0 * 160 : (r0 + 2) * 160], w, nt, preferred_element_type=F32)
                acc = t if acc is None else acc + t
            for r in range(2):
                ev[r0 + r, 8:168] = acc[r * 160 : (r + 1) * 160, :128]
                eg[r0 + r, 8:168] = acc[r * 160 : (r + 1) * 160, 128:]

        @pl.when(s >= 2)
        def _():
            put(s - 2).wait()

        lanes = pl.ds(pl.multiple_of(b * 128, 128), 128)
        taps = [
            [jnp.broadcast_to(cw[pl.ds(i * 2 + j, 1), lanes], (8, 128)) for i in range(9)] for j in range(2)
        ]
        step = 16
        for k in range(0, 160, step):
            sums = []
            for e, w in ((ev, taps[0]), (eg, taps[1])):
                acc = [None] * 4
                for r in range(6):
                    for bb in range(3):
                        v = e[r, k + 7 + bb : k + 7 + bb + step].reshape(step // 8, 8, 128)
                        for a in range(3):
                            o = r - a
                            if 0 <= o < 4:
                                t = (v * w[a * 3 + bb]).reshape(step, 128)
                                acc[o] = t if acc[o] is None else acc[o] + t
                sums.append(acc)
            for o in range(4):
                v, g = sums[0][o], sums[1][o]
                res = (0.5 * v * g) * (1.0 + jnp.tanh(0.5 * g))
                obuf[slot, o, k : k + step] = res.astype(BF16)
        put(s).start()
        return 0

    lax.fori_loop(0, 22, block, 0)
    put(20).wait()
    put(21).wait()
    out_copy.wait()
    for copy in halos:
        copy.wait_send()
    send(got, got, rs_s, rs_r, tm, h).wait_send()
    send(early, early, pre_s, pre_r, tm, h).wait_send()
    send(full.at[0:15], full.at[0:15], ag_s, ag_r, tm, h).wait_send()
    whole = w_all.at[0, 0, pl.ds(0, 15 * SHARD)]
    for sem in (ring_s, y_s, dr_s, dy_s):
        send(whole, whole, sem, ring_r.at[0], tm, h).wait_send()


def local(stream, query_tokens, key_tokens, value_tokens, out_weight, in_weight, conv_weight):
    height = lax.axis_index("height")
    heights = lax.axis_size("height")
    wt = in_weight.transpose(2, 1, 0)
    after = lax.ppermute(wt[:16], "height", [(i + 1, i) for i in range(heights - 1)])
    wt = lax.dynamic_slice(jnp.concatenate([wt, after]), (height, 0, 0), (SHARD, 2, 2240))
    wt = jnp.pad(wt, ((0, 0), (0, 0), (0, 64))).transpose(1, 0, 2)
    wp = jnp.stack([wt[:, :, :KH], wt[:, :, KH:]])
    cw = jnp.pad(conv_weight.reshape(18, 2800), ((0, 0), (0, 16)))
    anyspace = pl.BlockSpec(memory_space=pl.ANY)
    vmem = pl.BlockSpec(memory_space=pltpu.VMEM)
    dma, V = pltpu.SemaphoreType.DMA, pltpu.VMEM
    attended, gated, _ = pl.pallas_call(
        kernel,
        in_specs=[anyspace] * 5 + [vmem] * 2,
        out_specs=[anyspace] * 3,
        out_shape=[
            jax.ShapeDtypeStruct((TOK, COLS), BF16),
            jax.ShapeDtypeStruct((4, 160, CH), BF16),
            jax.ShapeDtypeStruct((2, 2, CH, KH), BF16),
        ],
        scratch_shapes=[
            V((960, COLS), BF16), V((960, 2240), BF16), V((TOK, COLS), BF16), V((TOK, COLS), BF16),
            V((COLS, 2240), BF16), V((960, COLS), BF16), V((2, 960, KH), BF16),
            V((16, 8, KH), F32), V((15, 8, KH), F32), V((8, KH), F32), V((7, 8, KH), F32), V((16, 8, KH), F32),
            V((5, 512, 256), BF16), V((5, 512, 256), BF16),
            V((6, 176, 128), F32), V((6, 176, 128), F32),
            V((2, 2, 2, 128, KH), BF16), V((2, 4, 160, 128), BF16),
            dma((5,)), dma((4,)), dma((4,)),
            dma, dma, dma, dma, dma, dma,
            dma, dma, dma, dma, dma((16,)), dma((16,)), dma((16,)), dma((16,)),
            dma, dma((2,)), dma((2,)), dma,
        ],
        compiler_params=pltpu.CompilerParams(
            collective_id=0, has_side_effects=True, vmem_limit_bytes=60 * 2**20
        ),
    )(
        query_tokens.reshape(TOK, COLS), key_tokens.reshape(TOK, COLS), value_tokens.reshape(TOK, COLS),
        stream.reshape(TOK, 2240), out_weight, wp, cw,
    )
    return attended.reshape(1, 4, 160, COLS), gated[None, :, :, :2800]


def solution(mesh):
    rows = P("tm", "height", None, None)
    return jax.shard_map(
        local,
        mesh=mesh,
        in_specs=(rows, rows, rows, rows, P(), P(None, None, "height"), P()),
        out_specs=(rows, rows),
        check_vma=False,
    )
```

time: 302 us -> 166 us (0.55)
  Pallas kernels: 0 us -> 147 us
  waiting for transfers between devices: 116 us -> 5.72 us
  matrix products: 45.4 us -> 0 us
  other arithmetic: 41.3 us -> 2.61 us
  local copies, waits for them, and re-layouts: 44.6 us -> 8.04 us
  starting transfers between devices: 23.2 us -> 1.29 us
  blocking collectives: 15.6 us -> 0 us
  between operations: 14.2 us -> 0.71 us
    pallas_call x0 -> x1, Pallas kernels: none -> 147 us  [local(): pl.pallas_call(kernel, in_specs=[anyspace] * 5 + [vmem] * 2, out_specs=[a...]
    all_gather x1 -> x0, waiting for transfers between devices: 61.3 us -> none  [local(): lax.all_gather(in_weight, 'height', axis=2, tiled=True)]
    dot_general x5 -> x0, matrix products: 45.4 us -> none  [the longest x1 25.4 us: local(): jnp.einsum('frwd,djc->frwjc', mixed, lax.all_gather(in_weight, 'height',...]
    ppermute x2 -> x1, waiting for transfers between devices: 32.1 us -> 5.72 us  [local(): lax.ppermute(wt[:16], 'height', [(i + 1, i) for i in range(heights - 1)])]
    all_to_all x3 -> x0, waiting for transfers between devices: 22 us -> none  [the longest x1 15.6 us: sent_and_summed(): lax.all_to_all(parts, axis, split_axis=0, concat_axis=0, tiled=True)]
    add x3 -> x0, other arithmetic: 18.7 us -> none  [the longest x1 18.5 us: depthwise(): total + padded[:, row_off:row_off + rows, col_off:col_off + columns].asty...]
    all_to_all x3 -> x0, starting transfers between devices: 17.9 us -> none  [the longest x2 9.3 us: sent_to_all(): return lax.all_to_all(copies, axis, split_axis=0, concat_axis=0, tiled=True)]
    another operation x4 -> x1, local copies, waits for them, and re-layouts: 17 us -> 0.13 us  [local(): wp = jnp.stack([wt[:, :, :KH], wt[:, :, KH:]])]
  transfers between devices with their start and end apart: 6 -> 1, of which waited for: 5 -> 1; matrix products, arithmetic and copies ran while one was open for 22% -> 1% of each run, Pallas kernels for 0% -> 0%
where the time goes in v2:
time: 166 us; the launch traced here: 165 us
  Pallas kernels  147 us (89%)
  local copies, waits for them, and re-layouts  8.04 us (5%)
  waiting for transfers between devices  5.72 us (3%)
  other arithmetic  2.61 us (2%)
    pallas_call x1, Pallas kernels, local(): pl.pallas_call(kernel, in_specs=[anyspace] * 5 + [vmem] * 2, out_specs=[a...  147 us
    ppermute x1, waiting for transfers between devices, local(): lax.ppermute(wt[:16], 'height', [(i + 1, i) for i in range(heights - 1)])  5.72 us
    broadcast_in_dim x1, local copies, waits for them, and re-layouts, local(): return (attended.reshape(1, 4, 160, COLS), gated[None, :, :, :2800])  4.18 us
  transfers between devices with their start and end apart: 1, of which 1 were waited for; matrix products, arithmetic and copies ran while one was open for 1% of the time, Pallas kernels for 0%

profile of v2, /device:TPU:1, one launch (start us, length us, event | category | flops | bytes accessed | tf_op | source)
XLA Modules:
  0.0 165.3 jit_solution(9402832479513992180)
XLA Ops:
  0.6 0.0 copy-start.1
  0.6 1.6 copy.11
  2.3 1.3 collective-permute-start
  3.6 0.0 copy-done.1
  3.6 0.1 reshape.26
  3.7 0.7 pad.9.cw
  4.5 5.7 %collective-permute-done = bf16[16,2,2240]{2,0,1:T(8,128)(2,1)S(1)} collective-permute-done((bf16[16,2,2240]{2,0,1:T(8,128)(2,1)S(1)}, bf16[16,2,2240]{2,0,1:T(8,128)(2,1)S(1)}, u32[]{:S(2)}, u32[]{:S(2)}) %collective-permute-start) | collective-permute-done | bytes 143392 | tf_op jit(solution)/shard_map/ppermute | solution.py:393
  10.2 1.3 fusion
  11.5 0.1 pad_bitcast_fusion
  11.6 0.1 slice_bitcast_fusion.2
  11.7 1.3 pad_maximum_fusion.wp
  13.1 146.9 %shard_map.86 = (bf16[640,1120]{1,0:T(8,128)(2,1)}, bf16[4,160,2816]{2,1,0:T(8,128)(2,1)}, bf16[2,2,2816,1152]{3,2,1,0:T(8,128)(2,1)}) custom-call(bf16[640,1120]{1,0:T(8,128)(2,1)} %bitcast.19, bf16[640,1120]{1,0:T(8,128)(2,1)} %bitcast.20, bf16[640,1120]{1,0:T(8,128)(2,1)} %bitcast.21, bf16[640,2240]{1,0:T(8,128)(2,1)} %bitcast.18, ...), custom_call_target="tpu_custom_call" | custom-call | tf_op jit(solution)/shard_map/pallas_call | solution.py:401
  160.0 0.0 copy-start
  160.0 4.2 %slice_bitcast_fusion = bf16[1,4,160,2800]{3,2,1,0:T(8,128)(2,1)} fusion(bf16[4,160,2816]{2,1,0:T(8,128)(2,1)} %get-tuple-element.5), kind=kLoop, calls=%fused_computation | loop fusion | bytes 7168000 | tf_op jit(solution)/shard_map/broadcast_in_dim | solution.py:429
  164.2 0.0 copy-done
  164.2 1.1 copy.13
  (1 shorter events, 0.0 us)
Async XLA Ops:
  0.6 3.0 %copy-start.1 = (f32[3,3,2,2800]{3,2,1,0:T(2,128)S(1)}, f32[3,3,2,2800]{3,2,1,0:T(2,128)}, u32[]{:S(2)}) copy-start(f32[3,3,2,2800]{3,2,1,0:T(2,128)} %param.13) | copy-start | bytes 604804
  2.3 7.9 %collective-permute-start = (bf16[16,2,2240]{2,0,1:T(8,128)(2,1)S(1)}, bf16[16,2,2240]{2,0,1:T(8,128)(2,1)S(1)}, u32[]{:S(2)}, u32[]{:S(2)}) collective-permute-start(bf16[16,2,2240]{2,0,1:T(8,128)(2,1)S(1)} %slice.16), channel_id=1, source_target_pairs={{1,0},{2,1},{3,2},{4,3},{5,4},{6,5},{7,6},{8,7},{9,8},{10,9},{11,1... | collective-permute-start | bytes 430088 | tf_op jit(solution)/shard_map/ppermute | solution.py:393
  160.0 4.2 %copy-start = (bf16[640,1120]{1,0:T(8,128)(2,1)S(1)}, bf16[640,1120]{1,0:T(8,128)(2,1)}, u32[]{:S(2)}) copy-start(bf16[640,1120]{1,0:T(8,128)(2,1)} %get-tuple-element.4) | copy-start | bytes 4300804

commit v3 on v2

--- a/solution.py
+++ b/solution.py
@@ -35,11 +35,11 @@
 
 
 def kernel(
-    q_h, k_h, v_h, s_h, ow_h, wp, cw,
+    q_h, k_h, v_h, s_h, ow_h, wa_h, wb_h, cw,
     att_out, gated_out, w_all,
-    q6, s6, kk, vv, ow, att, mix, own, got, tot, early, full, bd, hd, ev, eg, wbuf, obuf,
+    q6, s6, kk, vv, ow, wp, wx, att, mix, own, got, tot, early, full, bd, hd, ev, eg, wbuf, obuf,
     load_sem, halo_s, halo_r, rs_s, rs_r, pre_s, pre_r, ag_s, ag_r,
-    ring_s, y_s, dr_s, dy_s, ring_r, y_r, dr_r, dy_r, fill_sem, wb_sem, ob_sem, att_sem,
+    ring_s, y_s, dr_s, dy_s, ring_r, y_r, dr_r, dy_r, fill_sem, wb_sem, ob_sem, att_sem, edge_s, edge_r,
 ):
     tm, h = lax.axis_index("tm"), lax.axis_index("height")
     y, c = tm // 2, lax.rem(tm, 2)
@@ -50,9 +50,10 @@
     loads = [
         pltpu.make_async_copy(k_h, kk, load_sem.at[0]),
         pltpu.make_async_copy(v_h, vv, load_sem.at[1]),
-        pltpu.make_async_copy(q_h, q6.at[160:800], load_sem.at[2]),
-        pltpu.make_async_copy(s_h, s6.at[160:800], load_sem.at[3]),
+        pltpu.make_async_copy(q_h, q6.at[0:640], load_sem.at[2]),
+        pltpu.make_async_copy(s_h, s6.at[0:640], load_sem.at[3]),
         pltpu.make_async_copy(ow_h, ow, load_sem.at[4]),
+        pltpu.make_async_copy(wa_h, wp, load_sem.at[5]),
     ]
     fill = pltpu.make_async_copy(wp, w_all.at[:, :, pl.ds(pl.multiple_of(h * SHARD, 16), SHARD)], fill_sem)
 
@@ -68,10 +69,10 @@
 
     lax.fori_loop(1, 16, greet, 0)
     lax.fori_loop(1, 8, greet_tm, 0)
-    for copy in loads:
-        copy.start()
-    fill.start()
+    for i in (5, 0, 1, 2, 3, 4):
+        loads[i].start()
     pl.semaphore_wait(barrier, 22)
+    up, down = lax.rem(h + 15, 16), lax.rem(h + 1, 16)
 
     def send(src, dst, ssem, rsem, to_tm, to_h):
         return pltpu.make_async_remote_copy(
@@ -95,11 +96,12 @@
     def ring_wait(o):
         send(piece(o, c, j0), piece(o, c, j0), ring_s, ring_r.at[o], tm, h).wait_recv()
 
-    def pass_on(o):
-        low = lax.rem(o, 4) // 2
+    def pass_on(o, over_y=True):
+        low = lax.rem(o // 8 + lax.rem(o, 4) // 2, 2)
         yt = lax.rem(y + 3 + 2 * low, 4)
         p = piece(o, c, j0)
-        send(p, p, y_s, y_r.at[o], yt * 2 + c, h).start()
+        if over_y:
+            send(p, p, y_s, y_r.at[o], yt * 2 + c, h).start()
         send(p, p, dr_s, dr_r.at[o], y * 2 + 1 - c, h).start()
 
     def y_take(o):
@@ -117,19 +119,25 @@
         ring_send(o, at(1, z), src)
         ring_send(o, at(-1, z), src)
 
+    edge = send(wb_h, wx, edge_s, edge_r, tm, up)
+    edge.start()
+    own[...] = jnp.zeros(own.shape, BF16)
+    loads[5].wait()
+    edge.wait_recv()
+    wp[:, :, 160:176] = wp[:, :, 160:176] + wx[...]
+    loads[0].wait()
+    for r in range(0, TOK, 160):
+        kk[r : r + 160] = phi(kk[r : r + 160]).astype(BF16)
     mine = wp.at[c, j0]
     dz = 1 - 2 * c
     ring_send(h, x * 4 + zat(1), mine)
     ring_send(h, x * 4 + zat(-1), mine)
     to_x(h, mine)
-
-    own[...] = jnp.zeros(own.shape, F32)
-    loads[0].wait()
-    for r in range(0, TOK, 160):
-        kk[r : r + 160] = phi(kk[r : r + 160]).astype(BF16)
+    fill.start()
+
     loads[1].wait()
     norm = jnp.sum(kk[...].astype(F32), axis=0, keepdims=True)
-    own[14, :, :COLS] = jnp.broadcast_to(norm, (8, COLS))
+    own[14, :, :COLS] = jnp.broadcast_to(norm, (8, COLS)).astype(BF16)
     for t0, t1, w0, w1 in TILES:
         part = lax.dot_general(
             kk[:, w0:w1], vv[:, t0:t1], (((0,), (0,)), ((), ())), preferred_element_type=F32
@@ -138,7 +146,7 @@
         for head in heads_of(t0, t1):
             a = head * HD - w0
             state = jnp.where(lanes_in(head, t0, t1), part[a : a + HD], state)
-        own[0:14, :, t0:t1] = state.reshape(14, 8, t1 - t0)
+        own[0:14, :, t0:t1] = state.reshape(14, 8, t1 - t0).astype(BF16)
 
     def rs(d, _):
         to = lax.rem(h + d, 16)
@@ -148,31 +156,39 @@
     lax.fori_loop(1, 16, rs, 0)
 
     zm, zp, zf = x * 4 + zat(-1), x * 4 + zat(1), x * 4 + zat(2)
+    loads[2].wait()
+    for r in range(0, TOK, 160):
+        q6[r : r + 160] = phi(q6[r : r + 160]).astype(BF16)
     ring_wait(zm)
     ring_wait(zp)
     ring_send(x * 4 + zat(-dz), x * 4 + zat(dz))
-    to_x(zm)
-
-    loads[2].wait()
-    for r in range(160, 800, 160):
-        q6[r : r + 160] = phi(q6[r : r + 160]).astype(BF16)
 
     send(got, got, rs_s, rs_r, tm, h).wait_recv()
-    tot[...] = own[h] + jnp.sum(got[...], axis=0)
+    tot[...] = own[h].astype(F32) + jnp.sum(got[...].astype(F32), axis=0)
 
     def pre(d, _):
         send(tot, early.at[d - 1], pre_s, pre_r, lax.rem(tm + d, 8), h).start()
         return 0
 
     lax.fori_loop(1, 8, pre, 0)
-    to_x(zp)
+    halos = [
+        send(q_h.at[480:640], q6.at[640:800], halo_s.at[0], halo_r.at[0], tm, down),
+        send(q_h.at[0:160], q6.at[800:960], halo_s.at[1], halo_r.at[1], tm, up),
+        send(s_h.at[480:640], s6.at[640:800], halo_s.at[2], halo_r.at[2], tm, down),
+        send(s_h.at[0:160], s6.at[800:960], halo_s.at[3], halo_r.at[3], tm, up),
+    ]
+    halos[0].start()
+    halos[1].start()
     pass_on(zm)
     pass_on(zp)
     send(early, early, pre_s, pre_r, tm, h).wait_recv()
     causal = tot[...]
     for d in range(1, 8):
         causal = causal + jnp.where(d <= tm, early[d - 1], 0.0)
-    full[h] = causal
+    high = causal.astype(BF16)
+    rest = (causal - high.astype(F32)).astype(BF16)
+    odd = lax.broadcasted_iota(jnp.int32, causal.shape, 0) == 1
+    full[h] = jnp.where(odd & (h == 14), rest.astype(F32), high.astype(F32)).astype(BF16)
 
     def ag(d, _):
         to = lax.rem(h + d, 16)
@@ -180,20 +196,8 @@
         return 0
 
     lax.fori_loop(1, 16, ag, 0)
-
-    up, down = lax.rem(h + 15, 16), lax.rem(h + 1, 16)
-    halos = [
-        send(q_h.at[480:640], q6.at[0:160], halo_s.at[0], halo_r.at[0], tm, down),
-        send(q_h.at[0:160], q6.at[800:960], halo_s.at[1], halo_r.at[1], tm, up),
-        send(s_h.at[480:640], s6.at[0:160], halo_s.at[2], halo_r.at[2], tm, down),
-        send(s_h.at[0:160], s6.at[800:960], halo_s.at[3], halo_r.at[3], tm, up),
-    ]
-    for copy in halos:
-        copy.start()
-
-    ring_wait(zf)
-    to_x(zf)
-    pass_on(zf)
+    halos[2].start()
+    halos[3].start()
 
     def x_event(k):
         zz = zat(k)
@@ -201,25 +205,32 @@
         ring_wait(at(-1, zz))
         ring_wait(at(1, zz))
         ring_send(lax.rem(x - d + 4, 4) * 4 + zz, lax.rem(x + d + 4, 4) * 4 + z)
-        pass_on(at(-1, zz))
-        pass_on(at(1, zz))
+        pass_on(at(-1, zz), k != 0)
+        pass_on(at(1, zz), k != 0)
 
     def far_event(k):
         ring_wait(at(2, zat(k)))
         pass_on(at(2, zat(k)))
 
     x_event(0)
+    to_x(zm)
+    to_x(zp)
+    ring_wait(zf)
+    to_x(zf)
+    pass_on(zf)
+    for to in (at(1, z), at(-1, z)):
+        send(wp.at[c, j1], piece(h, c, j1), y_s, y_r.at[h], tm, to).start()
 
     send(full.at[0:15], full.at[0:15], ag_s, ag_r, tm, h).wait_recv()
     for i, (t0, t1, w0, w1) in enumerate(TILES):
         bd[i] = jnp.zeros(bd.shape[1:], BF16)
         hd[i] = jnp.zeros(hd.shape[1:], BF16)
-        state = full[0:14, :, t0:t1].reshape(HD, t1 - t0)
+        state = full[0:14, :, t0:t1].astype(F32).reshape(HD, t1 - t0)
         for head in heads_of(t0, t1):
             a, inside = head * HD - w0, lanes_in(head, t0, t1)
             bd[i, a : a + HD, : t1 - t0] = jnp.where(inside, state, 0.0).astype(BF16)
             hd[i, a : a + HD, : t1 - t0] = jnp.where(inside, 1.0, 0.0).astype(BF16)
-    norms = full[14, 0:1, :COLS]
+    norms = full[14, 0:1, :COLS].astype(F32) + full[14, 1:2, :COLS].astype(F32)
 
     def attend(r0, n):
         for i, (t0, t1, w0, w1) in enumerate(TILES):
@@ -232,36 +243,38 @@
             den = jnp.dot(qa, e, preferred_element_type=F32) + jnp.dot(qb, e, preferred_element_type=F32)
             att[r0 : r0 + n, t0:t1] = (num / den).astype(BF16)
 
-    def project(r0, n, keep=None):
+    def project(r0, n, edges=False):
         for kh in range(2):
             for a in range(0, KH, 256):
                 b = min(a + 256, KH if kh == 0 else 1088)
                 cols = slice(kh * KH + a, kh * KH + b)
                 p = jnp.dot(att[r0 : r0 + n], ow[:, cols], preferred_element_type=F32)
                 p = p + s6[r0 : r0 + n, cols].astype(F32)
-                if keep is not None:
-                    p = jnp.where(keep, p, 0.0)
+                if edges:
+                    p = jnp.concatenate([jnp.where(h > 0, p[:160], 0.0), jnp.where(h < 15, p[160:], 0.0)])
                 mix[kh, r0 : r0 + n, a:b] = p.astype(BF16)
         mix[1, r0 : r0 + n, 1088:KH] = jnp.zeros((n, KH - 1088), BF16)
 
-    attend(160, 640)
-    out_copy = pltpu.make_async_copy(att.at[160:800], att_out, att_sem)
+    attend(0, 640)
+    out_copy = pltpu.make_async_copy(att.at[0:640], att_out, att_sem)
     out_copy.start()
-    x_event(-1)
-    x_event(1)
     y_take(zm)
     y_take(zp)
+    far_event(0)
     loads[3].wait()
     loads[4].wait()
-    project(160, 640)
+    project(0, 640)
+    x_event(-1)
     y_take(zf)
-    x_event(2)
-    for copy in halos:
-        copy.wait_recv()
-    for r, keep in ((0, h > 0), (800, h < 15)):
+    halos[0].wait_recv()
+    halos[1].wait_recv()
+    for r in (640, 800):
         q6[r : r + 160] = phi(q6[r : r + 160]).astype(BF16)
-        attend(r, 160)
-        project(r, 160, keep)
+    attend(640, 320)
+    halos[2].wait_recv()
+    halos[3].wait_recv()
+    project(640, 320, True)
+    x_event(1)
 
     def block_of(s):
         g = s // 5
@@ -300,27 +313,30 @@
 
     def at_step(s):
         if s == 0:
-            y_take(at(-1, z)), y_take(at(1, z)), far_event(0)
+            y_take(at(-1, z)), y_take(at(1, z))
         elif s == 1:
+            far_event(-1)
+        elif s == 2:
             y_take(at(-1, zat(-1))), y_take(at(1, zat(-1)))
-        elif s == 2:
-            y_take(at(-1, zat(1))), y_take(at(1, zat(1))), far_event(-1)
         elif s == 3:
-            y_take(at(-1, zat(2))), y_take(at(1, zat(2))), far_event(1)
+            x_event(2)
         elif s == 4:
-            ready(1)
+            y_take(at(-1, zat(1))), y_take(at(1, zat(1))), far_event(1)
+            y_take(at(-1, zat(2))), y_take(at(1, zat(2))), ready(1)
         elif s == 6:
             far_event(2)
-        elif s == 8:
+        elif s == 7:
             y_take(at(2, z)), y_take(at(2, zat(-1)))
         elif s == 9:
             ready(-1)
+        elif s == 11:
+            y_take(at(2, zat(1)))
         elif s == 12:
-            y_take(at(2, zat(1))), y_take(at(2, zat(2)))
+            y_take(at(2, zat(2)))
         elif s == 14:
             ready(2)
 
-    events = (0, 1, 2, 3, 4, 6, 8, 9, 12, 14)
+    events = (0, 1, 2, 3, 4, 6, 7, 9, 11, 12, 14)
 
     def block(s, _):
         for e in events:
@@ -333,15 +349,15 @@
 
         fetch(s).wait()
         b = block_of(s)
-        for r0 in range(0, 6, 2):
+        for r0, pair in ((0, (1, 2)), (2, (3, 4)), (4, (0, 5))):
             acc = None
             for kh in range(2):
                 w = wbuf[slot, kh].reshape(256, KH)
                 t = lax.dot_general(mix[kh, r0 * 160 : (r0 + 2) * 160], w, nt, preferred_element_type=F32)
                 acc = t if acc is None else acc + t
-            for r in range(2):
-                ev[r0 + r, 8:168] = acc[r * 160 : (r + 1) * 160, :128]
-                eg[r0 + r, 8:168] = acc[r * 160 : (r + 1) * 160, 128:]
+            for i, r in enumerate(pair):
+                ev[r, 8:168] = acc[i * 160 : (i + 1) * 160, :128]
+                eg[r, 8:168] = acc[i * 160 : (i + 1) * 160, 128:]
 
         @pl.when(s >= 2)
         def _():
@@ -376,6 +392,7 @@
     put(20).wait()
     put(21).wait()
     out_copy.wait()
+    edge.wait_send()
     for copy in halos:
         copy.wait_send()
     send(got, got, rs_s, rs_r, tm, h).wait_send()
@@ -388,19 +405,17 @@
 
 def local(stream, query_tokens, key_tokens, value_tokens, out_weight, in_weight, conv_weight):
     height = lax.axis_index("height")
-    heights = lax.axis_size("height")
-    wt = in_weight.transpose(2, 1, 0)
-    after = lax.ppermute(wt[:16], "height", [(i + 1, i) for i in range(heights - 1)])
-    wt = lax.dynamic_slice(jnp.concatenate([wt, after]), (height, 0, 0), (SHARD, 2, 2240))
-    wt = jnp.pad(wt, ((0, 0), (0, 0), (0, 64))).transpose(1, 0, 2)
-    wp = jnp.stack([wt[:, :, :KH], wt[:, :, KH:]])
+    wt = jnp.pad(in_weight.transpose(2, 1, 0), ((16, 16), (0, 0), (0, 64)))
+    wt = wt.reshape(207, 2, 2, KH)
+    wa = lax.dynamic_slice(wt, (16 + height, 0, 0, 0), (SHARD, 2, 2, KH)).transpose(2, 1, 0, 3)
+    wb = lax.dynamic_slice(wt, (height, 0, 0, 0), (16, 2, 2, KH)).transpose(2, 1, 0, 3)
     cw = jnp.pad(conv_weight.reshape(18, 2800), ((0, 0), (0, 16)))
     anyspace = pl.BlockSpec(memory_space=pl.ANY)
     vmem = pl.BlockSpec(memory_space=pltpu.VMEM)
     dma, V = pltpu.SemaphoreType.DMA, pltpu.VMEM
     attended, gated, _ = pl.pallas_call(
         kernel,
-        in_specs=[anyspace] * 5 + [vmem] * 2,
+        in_specs=[anyspace] * 7 + [vmem],
         out_specs=[anyspace] * 3,
         out_shape=[
             jax.ShapeDtypeStruct((TOK, COLS), BF16),
@@ -409,22 +424,22 @@
         ],
         scratch_shapes=[
             V((960, COLS), BF16), V((960, 2240), BF16), V((TOK, COLS), BF16), V((TOK, COLS), BF16),
-            V((COLS, 2240), BF16), V((960, COLS), BF16), V((2, 960, KH), BF16),
-            V((16, 8, KH), F32), V((15, 8, KH), F32), V((8, KH), F32), V((7, 8, KH), F32), V((16, 8, KH), F32),
+            V((COLS, 2240), BF16), V((2, 2, SHARD, KH), BF16), V((2, 2, 16, KH), BF16), V((960, COLS), BF16), V((2, 960, KH), BF16),
+            V((16, 8, KH), BF16), V((15, 8, KH), BF16), V((8, KH), F32), V((7, 8, KH), F32), V((16, 8, KH), BF16),
             V((5, 512, 256), BF16), V((5, 512, 256), BF16),
             V((6, 176, 128), F32), V((6, 176, 128), F32),
             V((2, 2, 2, 128, KH), BF16), V((2, 4, 160, 128), BF16),
-            dma((5,)), dma((4,)), dma((4,)),
+            dma((6,)), dma((4,)), dma((4,)),
             dma, dma, dma, dma, dma, dma,
             dma, dma, dma, dma, dma((16,)), dma((16,)), dma((16,)), dma((16,)),
-            dma, dma((2,)), dma((2,)), dma,
+            dma, dma((2,)), dma((2,)), dma, dma, dma,
         ],
         compiler_params=pltpu.CompilerParams(
             collective_id=0, has_side_effects=True, vmem_limit_bytes=60 * 2**20
         ),
     )(
         query_tokens.reshape(TOK, COLS), key_tokens.reshape(TOK, COLS), value_tokens.reshape(TOK, COLS),
-        stream.reshape(TOK, 2240), out_weight, wp, cw,
+        stream.reshape(TOK, 2240), out_weight, wa, wb, cw,
     )
     return attended.reshape(1, 4, 160, COLS), gated[None, :, :, :2800]
 

time: 166 us -> 185 us (1.11)
  Pallas kernels: 147 us -> 163 us
  local copies, waits for them, and re-layouts: 8.04 us -> 20.7 us
  waiting for transfers between devices: 5.72 us -> 0 us
  other arithmetic: 2.61 us -> 0 us
    pallas_call x1, Pallas kernels: 147 us -> 163 us  [local(): pl.pallas_call(kernel, in_specs=[anyspace] * 7 + [vmem], out_specs=[anysp...]
    ppermute x1 -> x0, waiting for transfers between devices: 5.72 us -> none  [local(): lax.ppermute(wt[:16], 'height', [(i + 1, i) for i in range(heights - 1)])]
    reshape x0 -> x1, local copies, waits for them, and re-layouts: none -> 5.24 us  [local(): wt = wt.reshape(207, 2, 2, KH)]
    dynamic_slice x0 -> x2, local copies, waits for them, and re-layouts: none -> 3.56 us  [the longest x1 2.55 us: local(): lax.dynamic_slice(wt, (16 + height, 0, 0, 0), (SHARD, 2, 2, KH))]
    pad x0 -> x1, local copies, waits for them, and re-layouts: none -> 2.84 us  [local(): wt = jnp.pad(in_weight.transpose(2, 1, 0), ((16, 16), (0, 0), (0, 64)))]
  transfers between devices with their start and end apart: 1 -> 0, of which waited for: 1 -> 0; matrix products, arithmetic and copies ran while one was open for 1% -> 0% of each run, Pallas kernels for 0% -> 0%
where the time goes in v3:
time: 185 us; the launch traced here: 184 us
  Pallas kernels  163 us (88%)
  local copies, waits for them, and re-layouts  20.7 us (11%)
    pallas_call x1, Pallas kernels, local(): pl.pallas_call(kernel, in_specs=[anyspace] * 7 + [vmem], out_specs=[anysp...  163 us
    reshape x1, local copies, waits for them, and re-layouts, local(): wt = wt.reshape(207, 2, 2, KH)  5.24 us
    broadcast_in_dim x1, local copies, waits for them, and re-layouts, local(): return (attended.reshape(1, 4, 160, COLS), gated[None, :, :, :2800])  4.18 us

profile of v3, /device:TPU:1, one launch (start us, length us, event | category | flops | bytes accessed | tf_op | source)
XLA Modules:
  0.0 184.3 jit_solution(1596511874027851039)
XLA Ops:
  0.6 1.1 reshape.30
  1.7 0.7 pad.9.cw
  2.4 2.8 %pad.8 = bf16[207,2,2304]{2,1,0:T(2,128)(2,1)S(1)} pad(bf16[175,2,2240]{2,1,0:T(2,128)(2,1)} %bitcast.16, bf16[]{:T(256)} %constant.4.clone.1), padding=16_16x0_0x0_64 | pad | bytes 3475714 | tf_op jit(solution)/shard_map/jit(_pad)/pad | solution.py:408
  5.3 5.2 %reshape.32 = bf16[207,2,2,1152]{3,2,1,0:T(2,128)(2,1)} reshape(bf16[207,2,2304]{2,1,0:T(2,128)(2,1)S(1)} %pad.8) | data formatting | bytes 3815424 | tf_op jit(solution)/shard_map/reshape | solution.py:409
  10.5 1.0 constant_dynamic-slice_fusion
  11.5 2.5 %constant_dynamic-slice_fusion.1 = bf16[176,2,2,1152]{3,2,1,0:T(2,128)(2,1)S(1)} fusion(bf16[207,2,2,1152]{3,2,1,0:T(2,128)(2,1)} %reshape.32, s32[]{:T(128)S(6)} %select_n.6), kind=kLoop, calls=%fused_computation.4 | loop fusion | bytes 3244036 | tf_op jit(solution)/shard_map/dynamic_slice | solution.py:410
  14.1 1.3 copy.18
  15.4 0.7 copy.19
  16.1 162.9 %shard_map.86 = (bf16[640,1120]{1,0:T(8,128)(2,1)}, bf16[4,160,2816]{2,1,0:T(8,128)(2,1)}, bf16[2,2,2816,1152]{3,2,1,0:T(8,128)(2,1)}) custom-call(bf16[640,1120]{1,0:T(8,128)(2,1)} %bitcast.17, bf16[640,1120]{1,0:T(8,128)(2,1)} %bitcast.18, bf16[640,1120]{1,0:T(8,128)(2,1)} %bitcast.19, bf16[640,2240]{1,0:T(8,128)(2,1)} %bitcast.15, ...), custom_call_target="tpu_custom_call" | custom-call | tf_op jit(solution)/shard_map/pallas_call | solution.py:416
  179.0 0.0 copy-start
  179.0 4.2 %slice_bitcast_fusion = bf16[1,4,160,2800]{3,2,1,0:T(8,128)(2,1)} fusion(bf16[4,160,2816]{2,1,0:T(8,128)(2,1)} %get-tuple-element.5), kind=kLoop, calls=%fused_computation | loop fusion | bytes 7168000 | tf_op jit(solution)/shard_map/broadcast_in_dim | solution.py:444
  183.2 0.0 copy-done
  183.2 1.1 copy.21
Async XLA Ops:
  179.0 4.2 %copy-start = (bf16[640,1120]{1,0:T(8,128)(2,1)S(1)}, bf16[640,1120]{1,0:T(8,128)(2,1)}, u32[]{:S(2)}) copy-start(bf16[640,1120]{1,0:T(8,128)(2,1)} %get-tuple-element.4) | copy-start | bytes 4300804

commit v4 on v3

--- a/solution.py
+++ b/solution.py
@@ -37,7 +37,7 @@
 def kernel(
     q_h, k_h, v_h, s_h, ow_h, wa_h, wb_h, cw,
     att_out, gated_out, w_all,
-    q6, s6, kk, vv, ow, wp, wx, att, mix, own, got, tot, early, full, bd, hd, ev, eg, wbuf, obuf,
+    q6, s6, kk, kt, vv, ow, wp, wx, att, mix, own, got, tot, early, full, bd, hd, ev, eg, wbuf, obuf,
     load_sem, halo_s, halo_r, rs_s, rs_r, pre_s, pre_r, ag_s, ag_r,
     ring_s, y_s, dr_s, dy_s, ring_r, y_r, dr_r, dy_r, fill_sem, wb_sem, ob_sem, att_sem, edge_s, edge_r,
 ):
@@ -118,6 +118,23 @@
     def to_x(o, src=None):
         ring_send(o, at(1, z), src)
         ring_send(o, at(-1, z), src)
+
+    def x_take(k):
+        zz = zat(k)
+        ring_wait(at(-1, zz))
+        ring_wait(at(1, zz))
+        pass_on(at(-1, zz))
+        pass_on(at(1, zz))
+
+    def x_turn(k):
+        zz = zat(k)
+        limit = jnp.where(z == 0, 3, jnp.where(z == 3, 1, 2))
+        d = jnp.where(zz < limit, 1, -1)
+        ring_send(lax.rem(x - d + 4, 4) * 4 + zz, lax.rem(x + d + 4, 4) * 4 + z)
+
+    def x_event(k):
+        x_take(k)
+        x_turn(k)
 
     edge = send(wb_h, wx, edge_s, edge_r, tm, up)
     edge.start()
@@ -133,15 +150,19 @@
     ring_send(h, x * 4 + zat(1), mine)
     ring_send(h, x * 4 + zat(-1), mine)
     to_x(h, mine)
+    for d in (1, -1):
+        send(wp.at[c, j1], piece(h, c, j1), y_s, y_r.at[h], tm, x * 4 + zat(d)).start()
     fill.start()
 
     loads[1].wait()
     norm = jnp.sum(kk[...].astype(F32), axis=0, keepdims=True)
     own[14, :, :COLS] = jnp.broadcast_to(norm, (8, COLS)).astype(BF16)
-    for t0, t1, w0, w1 in TILES:
-        part = lax.dot_general(
-            kk[:, w0:w1], vv[:, t0:t1], (((0,), (0,)), ((), ())), preferred_element_type=F32
-        )
+    for a in range(0, COLS, 128):
+        b = min(a + 128, COLS)
+        kt[a:b] = kk[:, a:b].T
+    zm, zp, zf = x * 4 + zat(-1), x * 4 + zat(1), x * 4 + zat(2)
+    for i, (t0, t1, w0, w1) in enumerate(TILES):
+        part = jnp.dot(kt[w0:w1], vv[:, t0:t1], preferred_element_type=F32)
         state = jnp.zeros((HD, t1 - t0), F32)
         for head in heads_of(t0, t1):
             a = head * HD - w0
@@ -154,14 +175,22 @@
         return 0
 
     lax.fori_loop(1, 16, rs, 0)
-
-    zm, zp, zf = x * 4 + zat(-1), x * 4 + zat(1), x * 4 + zat(2)
+    ring_wait(zm)
+    ring_wait(zp)
+    ring_send(x * 4 + zat(-dz), x * 4 + zat(dz))
+    to_x(zm)
+    pass_on(zm, False)
+    x_take(0)
+
+    to_x(zp)
+    pass_on(zp, False)
+    y_take(zm)
+    y_take(zp)
+    turn = piece(x * 4 + zat(-dz), c, j1)
+    send(turn, turn, y_s, y_r.at[x * 4 + zat(-dz)], tm, x * 4 + zat(dz)).start()
     loads[2].wait()
     for r in range(0, TOK, 160):
         q6[r : r + 160] = phi(q6[r : r + 160]).astype(BF16)
-    ring_wait(zm)
-    ring_wait(zp)
-    ring_send(x * 4 + zat(-dz), x * 4 + zat(dz))
 
     send(got, got, rs_s, rs_r, tm, h).wait_recv()
     tot[...] = own[h].astype(F32) + jnp.sum(got[...].astype(F32), axis=0)
@@ -179,8 +208,7 @@
     ]
     halos[0].start()
     halos[1].start()
-    pass_on(zm)
-    pass_on(zp)
+    x_take(-1)
     send(early, early, pre_s, pre_r, tm, h).wait_recv()
     causal = tot[...]
     for d in range(1, 8):
@@ -199,27 +227,16 @@
     halos[2].start()
     halos[3].start()
 
-    def x_event(k):
-        zz = zat(k)
-        d = 1 - 2 * (zz // 2)
-        ring_wait(at(-1, zz))
-        ring_wait(at(1, zz))
-        ring_send(lax.rem(x - d + 4, 4) * 4 + zz, lax.rem(x + d + 4, 4) * 4 + z)
-        pass_on(at(-1, zz), k != 0)
-        pass_on(at(1, zz), k != 0)
-
     def far_event(k):
         ring_wait(at(2, zat(k)))
         pass_on(at(2, zat(k)))
 
-    x_event(0)
-    to_x(zm)
-    to_x(zp)
+    x_turn(0)
+    x_turn(-1)
     ring_wait(zf)
     to_x(zf)
-    pass_on(zf)
-    for to in (at(1, z), at(-1, z)):
-        send(wp.at[c, j1], piece(h, c, j1), y_s, y_r.at[h], tm, to).start()
+    pass_on(zf, False)
+    x_event(1)
 
     send(full.at[0:15], full.at[0:15], ag_s, ag_r, tm, h).wait_recv()
     for i, (t0, t1, w0, w1) in enumerate(TILES):
@@ -258,23 +275,24 @@
     attend(0, 640)
     out_copy = pltpu.make_async_copy(att.at[0:640], att_out, att_sem)
     out_copy.start()
-    y_take(zm)
-    y_take(zp)
     far_event(0)
     loads[3].wait()
     loads[4].wait()
     project(0, 640)
-    x_event(-1)
+    far_event(-1)
+    x_event(2)
     y_take(zf)
+    y_take(at(-1, z)), y_take(at(1, z))
     halos[0].wait_recv()
     halos[1].wait_recv()
     for r in (640, 800):
         q6[r : r + 160] = phi(q6[r : r + 160]).astype(BF16)
     attend(640, 320)
+    far_event(1)
+    y_take(at(-1, zat(-1))), y_take(at(1, zat(-1)))
     halos[2].wait_recv()
     halos[3].wait_recv()
     project(640, 320, True)
-    x_event(1)
 
     def block_of(s):
         g = s // 5
@@ -312,31 +330,24 @@
             d_wait(at(dx, zat(k)))
 
     def at_step(s):
-        if s == 0:
-            y_take(at(-1, z)), y_take(at(1, z))
-        elif s == 1:
-            far_event(-1)
+        if s == 1:
+            y_take(at(-1, zat(1))), y_take(at(1, zat(1)))
         elif s == 2:
-            y_take(at(-1, zat(-1))), y_take(at(1, zat(-1)))
-        elif s == 3:
-            x_event(2)
+            far_event(2)
         elif s == 4:
-            y_take(at(-1, zat(1))), y_take(at(1, zat(1))), far_event(1)
             y_take(at(-1, zat(2))), y_take(at(1, zat(2))), ready(1)
         elif s == 6:
-            far_event(2)
-        elif s == 7:
             y_take(at(2, z)), y_take(at(2, zat(-1)))
         elif s == 9:
             ready(-1)
-        elif s == 11:
+        elif s == 10:
             y_take(at(2, zat(1)))
         elif s == 12:
             y_take(at(2, zat(2)))
         elif s == 14:
             ready(2)
 
-    events = (0, 1, 2, 3, 4, 6, 7, 9, 11, 12, 14)
+    events = (1, 2, 4, 6, 9, 10, 12, 14)
 
     def block(s, _):
         for e in events:
@@ -405,10 +416,15 @@
 
 def local(stream, query_tokens, key_tokens, value_tokens, out_weight, in_weight, conv_weight):
     height = lax.axis_index("height")
-    wt = jnp.pad(in_weight.transpose(2, 1, 0), ((16, 16), (0, 0), (0, 64)))
-    wt = wt.reshape(207, 2, 2, KH)
-    wa = lax.dynamic_slice(wt, (16 + height, 0, 0, 0), (SHARD, 2, 2, KH)).transpose(2, 1, 0, 3)
-    wb = lax.dynamic_slice(wt, (height, 0, 0, 0), (16, 2, 2, KH)).transpose(2, 1, 0, 3)
+    raw = in_weight.transpose(2, 1, 0)
+    blank = jnp.zeros((16, 2, 2240), BF16)
+
+    def packed(rows):
+        rows = jnp.pad(rows, ((0, 0), (0, 0), (0, 64))).transpose(1, 0, 2)
+        return jnp.stack([rows[:, :, :KH], rows[:, :, KH:]])
+
+    wa = packed(lax.dynamic_slice(jnp.concatenate([raw, blank]), (height, 0, 0), (SHARD, 2, 2240)))
+    wb = packed(lax.dynamic_slice(jnp.concatenate([blank, raw[:16]]), (height, 0, 0), (16, 2, 2240)))
     cw = jnp.pad(conv_weight.reshape(18, 2800), ((0, 0), (0, 16)))
     anyspace = pl.BlockSpec(memory_space=pl.ANY)
     vmem = pl.BlockSpec(memory_space=pltpu.VMEM)
@@ -423,7 +439,7 @@
             jax.ShapeDtypeStruct((2, 2, CH, KH), BF16),
         ],
         scratch_shapes=[
-            V((960, COLS), BF16), V((960, 2240), BF16), V((TOK, COLS), BF16), V((TOK, COLS), BF16),
+            V((960, COLS), BF16), V((960, 2240), BF16), V((TOK, COLS), BF16), V((COLS, TOK), BF16), V((TOK, COLS), BF16),
             V((COLS, 2240), BF16), V((2, 2, SHARD, KH), BF16), V((2, 2, 16, KH), BF16), V((960, COLS), BF16), V((2, 960, KH), BF16),
             V((16, 8, KH), BF16), V((15, 8, KH), BF16), V((8, KH), F32), V((7, 8, KH), F32), V((16, 8, KH), BF16),
             V((5, 512, 256), BF16), V((5, 512, 256), BF16),

time: 185 us -> 158 us (0.85)
  Pallas kernels: 163 us -> 146 us
  local copies, waits for them, and re-layouts: 20.7 us -> 9.57 us
  other arithmetic: 0 us -> 2.01 us
    pallas_call x1, Pallas kernels: 163 us -> 146 us  [local(): pl.pallas_call(kernel, in_specs=[anyspace] * 7 + [vmem], out_specs=[anysp...]
    reshape x1 -> x0, local copies, waits for them, and re-layouts: 5.24 us -> none  [local(): wt = wt.reshape(207, 2, 2, KH)]
    dynamic_slice x2, local copies, waits for them, and re-layouts: 3.56 us -> 0.61 us  [the longest x1 0.54 us: local(): lax.dynamic_slice(jnp.concatenate([raw, blank]), (height, 0, 0), (SHARD,...]
    pad x1 -> x0, local copies, waits for them, and re-layouts: 2.84 us -> none  [local(): wt = jnp.pad(in_weight.transpose(2, 1, 0), ((16, 16), (0, 0), (0, 64)))]
    another operation x0 -> x2, other arithmetic: none -> 2.01 us  [packed(): return jnp.stack([rows[:, :, :KH], rows[:, :, KH:]])]
where the time goes in v4:
time: 158 us
  Pallas kernels  146 us (92%)
  local copies, waits for them, and re-layouts  9.57 us (6%)
  other arithmetic  2.01 us (1%)
    pallas_call x1, Pallas kernels, local(): pl.pallas_call(kernel, in_specs=[anyspace] * 7 + [vmem], out_specs=[anysp...  146 us
    broadcast_in_dim x1, local copies, waits for them, and re-layouts, local(): return (attended.reshape(1, 4, 160, COLS), gated[None, :, :, :2800])  4.18 us

profile of v4, /device:TPU:1, one launch (start us, length us, event | category | flops | bytes accessed | tf_op | source)
XLA Modules:
  0.0 157.8 jit_solution(6771574002080957127)
XLA Ops:
  0.6 1.1 reshape.26
  1.7 0.7 pad.16.cw
  2.4 1.6 %copy.11 = bf16[2240,2,175]{0,2,1:T(8,128)(2,1)S(1)} copy(bf16[2240,2,175]{0,1,2:T(2,128)(2,1)} %param.12) | data formatting | bytes 3136000 | tf_op args[5]
  4.0 0.5 pad_dynamic-slice_fusion
  4.6 0.1 pad_dynamic-slice_fusion.1
  4.7 0.1 pad_bitcast_fusion
  4.8 0.1 slice_bitcast_fusion.2
  4.9 1.3 pad_maximum_fusion.wa_h
  6.3 0.7 pad_maximum_fusion.1.wb_h
  7.0 145.6 %shard_map.86 = (bf16[640,1120]{1,0:T(8,128)(2,1)}, bf16[4,160,2816]{2,1,0:T(8,128)(2,1)}, bf16[2,2,2816,1152]{3,2,1,0:T(8,128)(2,1)}) custom-call(bf16[640,1120]{1,0:T(8,128)(2,1)} %bitcast.25, bf16[640,1120]{1,0:T(8,128)(2,1)} %bitcast.26, bf16[640,1120]{1,0:T(8,128)(2,1)} %bitcast.27, bf16[640,2240]{1,0:T(8,128)(2,1)} %bitcast.24, ...), custom_call_target="tpu_custom_call" | custom-call | tf_op jit(solution)/shard_map/pallas_call | solution.py:432
  152.5 0.0 copy-start
  152.6 4.2 %slice_bitcast_fusion = bf16[1,4,160,2800]{3,2,1,0:T(8,128)(2,1)} fusion(bf16[4,160,2816]{2,1,0:T(8,128)(2,1)} %get-tuple-element.5), kind=kLoop, calls=%fused_computation | loop fusion | bytes 7168000 | tf_op jit(solution)/shard_map/broadcast_in_dim | solution.py:460
  156.7 0.0 copy-done
  156.7 1.1 copy.13
  (3 shorter events, 0.0 us)
Async XLA Ops:
  152.5 4.2 %copy-start = (bf16[640,1120]{1,0:T(8,128)(2,1)S(1)}, bf16[640,1120]{1,0:T(8,128)(2,1)}, u32[]{:S(2)}) copy-start(bf16[640,1120]{1,0:T(8,128)(2,1)} %get-tuple-element.4) | copy-start | bytes 4300804

commit v5 on v4

--- a/solution.py
+++ b/solution.py
@@ -162,6 +162,14 @@
         kt[a:b] = kk[:, a:b].T
     zm, zp, zf = x * 4 + zat(-1), x * 4 + zat(1), x * 4 + zat(2)
     for i, (t0, t1, w0, w1) in enumerate(TILES):
+        if i == 2:
+            ring_wait(zm)
+            ring_wait(zp)
+            ring_send(x * 4 + zat(-dz), x * 4 + zat(dz))
+            x_take(0)
+            x_turn(0)
+            to_x(zm)
+            pass_on(zm, False)
         part = jnp.dot(kt[w0:w1], vv[:, t0:t1], preferred_element_type=F32)
         state = jnp.zeros((HD, t1 - t0), F32)
         for head in heads_of(t0, t1):
@@ -175,12 +183,6 @@
         return 0
 
     lax.fori_loop(1, 16, rs, 0)
-    ring_wait(zm)
-    ring_wait(zp)
-    ring_send(x * 4 + zat(-dz), x * 4 + zat(dz))
-    to_x(zm)
-    pass_on(zm, False)
-    x_take(0)
 
     to_x(zp)
     pass_on(zp, False)
@@ -231,7 +233,6 @@
         ring_wait(at(2, zat(k)))
         pass_on(at(2, zat(k)))
 
-    x_turn(0)
     x_turn(-1)
     ring_wait(zf)
     to_x(zf)

time: 158 us -> 166 us (1.051)
  Pallas kernels: 146 us -> 153 us
    pallas_call x1, Pallas kernels: 146 us -> 153 us  [local(): pl.pallas_call(kernel, in_specs=[anyspace] * 7 + [vmem], out_specs=[anysp...]
where the time goes in v5:
time: 166 us; the launch traced here: 165 us
  Pallas kernels  153 us (92%)
  local copies, waits for them, and re-layouts  9.57 us (6%)
  other arithmetic  2.01 us (1%)
    pallas_call x1, Pallas kernels, local(): pl.pallas_call(kernel, in_specs=[anyspace] * 7 + [vmem], out_specs=[anysp...  153 us
    broadcast_in_dim x1, local copies, waits for them, and re-layouts, local(): return (attended.reshape(1, 4, 160, COLS), gated[None, :, :, :2800])  4.18 us

profile of v5, /device:TPU:1, one launch (start us, length us, event | category | flops | bytes accessed | tf_op | source)
XLA Modules:
  0.0 165.4 jit_solution(1573339242241816989)
XLA Ops:
  0.6 1.1 reshape.26
  1.7 0.7 pad.16.cw
  2.4 1.6 copy.11
  4.0 0.5 pad_dynamic-slice_fusion
  4.6 0.1 pad_dynamic-slice_fusion.1
  4.7 0.1 pad_bitcast_fusion
  4.8 0.1 slice_bitcast_fusion.2
  4.9 1.3 pad_maximum_fusion.wa_h
  6.3 0.7 pad_maximum_fusion.1.wb_h
  7.0 153.2 %shard_map.86 = (bf16[640,1120]{1,0:T(8,128)(2,1)}, bf16[4,160,2816]{2,1,0:T(8,128)(2,1)}, bf16[2,2,2816,1152]{3,2,1,0:T(8,128)(2,1)}) custom-call(bf16[640,1120]{1,0:T(8,128)(2,1)} %bitcast.25, bf16[640,1120]{1,0:T(8,128)(2,1)} %bitcast.26, bf16[640,1120]{1,0:T(8,128)(2,1)} %bitcast.27, bf16[640,2240]{1,0:T(8,128)(2,1)} %bitcast.24, ...), custom_call_target="tpu_custom_call" | custom-call | tf_op jit(solution)/shard_map/pallas_call | solution.py:433
  160.1 0.0 copy-start
  160.2 4.2 %slice_bitcast_fusion = bf16[1,4,160,2800]{3,2,1,0:T(8,128)(2,1)} fusion(bf16[4,160,2816]{2,1,0:T(8,128)(2,1)} %get-tuple-element.5), kind=kLoop, calls=%fused_computation | loop fusion | bytes 7168000 | tf_op jit(solution)/shard_map/broadcast_in_dim | solution.py:461
  164.3 0.0 copy-done
  164.3 1.1 copy.13
  (3 shorter events, 0.0 us)
Async XLA Ops:
  160.1 4.2 %copy-start = (bf16[640,1120]{1,0:T(8,128)(2,1)S(1)}, bf16[640,1120]{1,0:T(8,128)(2,1)}, u32[]{:S(2)}) copy-start(bf16[640,1120]{1,0:T(8,128)(2,1)} %get-tuple-element.4) | copy-start | bytes 4300804
